TPU v7x, 32 devices: a whole 2x2x4 slice. The times are simulated.
32 devices in a mesh: groups: 2 (over x), dates: 16 (over z, y, core).
Axes of the slice: x: 2, y: 2, z: 4, core: 2. Of those that a mesh axis runs over, the one named last changes fastest.
Arguments:
- scenes: bfloat16 [64, 4, 64, 128], P(('groups', 'dates')), parts along dimension 0, may hold values from -10 to 14
- cloud_mask: int32 [64, 64, 128], P(('groups', 'dates')), parts along dimension 0, may hold values 0 or 1
- region: int32 [128, 128], P('groups'), parts along dimension 0, may hold values from 0 to 7
Outputs:
- smoothed: bfloat16 [64, 4, 64, 128], P('groups', None, 'dates'), parts along dimension 0
- similarity: float32 [64, 32], P(('groups', 'dates')), parts along dimension 0
There are 2 independent parts, one for each index of `groups`. A program takes and returns all parts, laid end to end along the dimension named above; each array names one. Nothing has to cross between parts.
All inputs are finite; a program needn't handle non-finite values. No bound on the sum of `cloud_mask` on one device may be relied on, other than what follows from the above.
Results may differ from a plain program's by a relative error of at most 0.0065.
Values may be sent and summed in bfloat16 or wider, within the bound.
No kernel may reach another device: no remote copies, remote signals or barrier semaphores. Data moves between devices by JAX's collectives and lax.ppermute only.
A program may use at most 64 MiB of HBM per device.

v0:
```python
import jax
import jax.numpy as jnp
from jax import lax
from jax.sharding import PartitionSpec as P

REGIONS = 8
STEPS = 4


lam_space = 0.2
lam_time = 0.08


def extended(block, sides, width):
    for axis, dim in sides:
        count = lax.axis_size(axis)
        forward = [(i, i + 1) for i in range(count - 1)]
        backward = [(target, source) for source, target in forward]
        low = lax.ppermute(
            lax.slice_in_dim(block, block.shape[dim] - width, None, axis=dim), axis, forward
        )
        high = lax.ppermute(lax.slice_in_dim(block, 0, width, axis=dim), axis, backward)
        block = jnp.concatenate([low, block, high], axis=dim)
    return block


def edge_flux(difference):
    return difference / (1.0 + difference * difference)


def advance(current, padded_rows, padded_dates, row_weight, col_weight, date_weight):
    row_flux = lam_space * row_weight * edge_flux(padded_rows[:, :, 1:] - padded_rows[:, :, :-1])
    padded_cols = jnp.pad(current, ((0, 0), (0, 0), (0, 0), (1, 1)))
    col_flux = lam_space * col_weight * edge_flux(padded_cols[..., 1:] - padded_cols[..., :-1])
    date_flux = (
        lam_time
        * date_weight[:, None, None, None]
        * edge_flux(padded_dates[1:] - padded_dates[:-1])
    )
    return (
        current
        + (row_flux[:, :, 1:] - row_flux[:, :, :-1])
        + (col_flux[..., 1:] - col_flux[..., :-1])
        + (date_flux[1:] - date_flux[:-1])
    )


def local(scenes, cloud_mask, region):
    date_dev = scenes.shape[0]
    devices = lax.axis_size("dates")
    dates_all = date_dev * devices
    clear_half = cloud_mask.astype(jnp.bfloat16)
    masked = scenes * clear_half[:, None]
    labels = lax.broadcasted_iota(jnp.int32, (REGIONS, 1, 1), 0)
    member = region[None] == labels
    onehot_half = member.astype(jnp.bfloat16)
    onehot_full = member.astype(jnp.float32)
    sums = jnp.einsum("dbrc,grc->dbg", masked, onehot_half, preferred_element_type=jnp.float32)
    counts = jnp.einsum("drc,grc->dg", clear_half, onehot_half, preferred_element_type=jnp.float32)
    means = sums / (counts[:, None, :] + 1.0)
    pixel_mean = jnp.einsum("dbg,grc->dbrc", means, onehot_full, precision=lax.Precision.HIGHEST)
    anomaly = (
        cloud_mask.astype(jnp.float32)[:, None] * (scenes.astype(jnp.float32) - pixel_mean)
    ).astype(jnp.bfloat16)
    land_padded = jnp.pad((region > 0).astype(jnp.float32), 1)
    row_weight = land_padded[1:, 1:-1] * land_padded[:-1, 1:-1]
    col_weight = land_padded[1:-1, 1:] * land_padded[1:-1, :-1]
    lower = jnp.arange(date_dev + 1, dtype=jnp.int32) + lax.axis_index("dates") * date_dev - 1
    date_weight = ((lower >= 0) & (lower + 1 <= dates_all - 1)).astype(jnp.float32)
    current = anomaly.astype(jnp.float32)
    for step_index in range(STEPS):
        padded_dates = extended(current.astype(jnp.bfloat16), (("dates", 0),), 1).astype(
            current.dtype
        )
        padded_rows = jnp.pad(current, ((0, 0), (0, 0), (1, 1), (0, 0)))
        current = advance(current, padded_rows, padded_dates, row_weight, col_weight, date_weight)
    smoothed = lax.all_to_all(
        current.astype(jnp.bfloat16), "dates", split_axis=2, concat_axis=0, tiled=True
    )
    flat = smoothed.reshape(smoothed.shape[0], -1)
    total_features = flat.shape[1] * devices
    product = lax.dot_general(
        flat, flat, (((1,), (1,)), ((), ())), preferred_element_type=jnp.float32
    )
    similarity = lax.psum_scatter(
        product / total_features, "dates", scatter_dimension=0, tiled=True
    )
    return (smoothed, similarity)


def solution(mesh):
    in_specs = (
        P(("groups", "dates"), None, None, None),
        P(("groups", "dates"), None, None),
        P("groups", None),
    )
    out_specs = (P("groups", None, "dates", None), P(("groups", "dates"), None))
    return jax.shard_map(local, mesh=mesh, in_specs=in_specs, out_specs=out_specs, check_vma=False)
```

profile of v0, /device:TPU:0, one launch (start us, length us, event | category | flops | bytes accessed | tf_op | source)
XLA Modules:
  0.0 115.5 jit_solution(15377025040289881221)
XLA Ops:
  0.6 0.9 fusion.55
  1.6 0.7 copy-done.2
  2.5 0.4 fusion.3
  2.9 0.4 fusion.56
  3.3 2.4 %collective-permute-start = (bf16[1,4,64,128]{3,1,2,0:T(4,128)(2,1)S(1)}, bf16[1,4,64,128]{3,1,2,0:T(4,128)(2,1)S(1)}, u32[]{:S(2)}, u32[]{:S(2)}) collective-permute-start(bf16[1,4,64,128]{3,1,2,0:T(4,128)(2,1)S(1)} %get-tuple-element.16), channel_id=1, source_target_pairs={{0,1},{1,2},{2,3},{3,4},{4,5},{5,6},{6,7},{7,8},{8,9},{9,10},{10,1... | collective-permute-start | bytes 196616 | tf_op jit(solution)/shard_map/ppermute | solution.py:19
  5.7 1.3 %collective-permute-start.1 = (bf16[1,4,64,128]{3,1,2,0:T(4,128)(2,1)S(1)}, bf16[1,4,64,128]{3,1,2,0:T(4,128)(2,1)S(1)}, u32[]{:S(2)}, u32[]{:S(2)}) collective-permute-start(bf16[1,4,64,128]{3,1,2,0:T(4,128)(2,1)S(1)} %get-tuple-element.17), channel_id=1, source_target_pairs={{1,0},{2,1},{3,2},{4,3},{5,4},{6,5},{7,6},{8,7},{9,8},{10,9},{11,1... | collective-permute-start | bytes 196616 | tf_op jit(solution)/shard_map/ppermute | solution.py:22
  7.8 3.2 %collective-permute-done.1 = bf16[1,4,64,128]{3,1,2,0:T(4,128)(2,1)S(1)} collective-permute-done((bf16[1,4,64,128]{3,1,2,0:T(4,128)(2,1)S(1)}, bf16[1,4,64,128]{3,1,2,0:T(4,128)(2,1)S(1)}, u32[]{:S(2)}, u32[]{:S(2)}) %collective-permute-start.1) | collective-permute-done | bytes 65568 | tf_op jit(solution)/shard_map/ppermute | solution.py:22
  11.7 4.8 %collective-permute-start.2 = (bf16[1,4,64,128]{3,1,2,0:T(4,128)(2,1)S(1)}, bf16[1,4,64,128]{3,1,2,0:T(4,128)(2,1)S(1)}, u32[]{:S(2)}, u32[]{:S(2)}) collective-permute-start(bf16[1,4,64,128]{3,1,2,0:T(4,128)(2,1)S(1)} %get-tuple-element.14), channel_id=1, source_target_pairs={{0,1},{1,2},{2,3},{3,4},{4,5},{5,6},{6,7},{7,8},{8,9},{9,10},{10,1... | collective-permute-start | bytes 196616 | tf_op jit(solution)/shard_map/ppermute | solution.py:19
  16.5 1.3 %collective-permute-start.3 = (bf16[1,4,64,128]{3,1,2,0:T(4,128)(2,1)S(1)}, bf16[1,4,64,128]{3,1,2,0:T(4,128)(2,1)S(1)}, u32[]{:S(2)}, u32[]{:S(2)}) collective-permute-start(bf16[1,4,64,128]{3,1,2,0:T(4,128)(2,1)S(1)} %get-tuple-element.15), channel_id=1, source_target_pairs={{1,0},{2,1},{3,2},{4,3},{5,4},{6,5},{7,6},{8,7},{9,8},{10,9},{11,1... | collective-permute-start | bytes 196616 | tf_op jit(solution)/shard_map/ppermute | solution.py:22
  18.3 1.4 %collective-permute-done.3 = bf16[1,4,64,128]{3,1,2,0:T(4,128)(2,1)S(1)} collective-permute-done((bf16[1,4,64,128]{3,1,2,0:T(4,128)(2,1)S(1)}, bf16[1,4,64,128]{3,1,2,0:T(4,128)(2,1)S(1)}, u32[]{:S(2)}, u32[]{:S(2)}) %collective-permute-start.3) | collective-permute-done | bytes 65568 | tf_op jit(solution)/shard_map/ppermute | solution.py:22
  20.4 5.1 %collective-permute-start.4 = (bf16[1,4,64,128]{3,1,2,0:T(4,128)(2,1)S(1)}, bf16[1,4,64,128]{3,1,2,0:T(4,128)(2,1)S(1)}, u32[]{:S(2)}, u32[]{:S(2)}) collective-permute-start(bf16[1,4,64,128]{3,1,2,0:T(4,128)(2,1)S(1)} %get-tuple-element.12), channel_id=1, source_target_pairs={{0,1},{1,2},{2,3},{3,4},{4,5},{5,6},{6,7},{7,8},{8,9},{9,10},{10,1... | collective-permute-start | bytes 196616 | tf_op jit(solution)/shard_map/ppermute | solution.py:19
  25.5 1.3 %collective-permute-start.5 = (bf16[1,4,64,128]{3,1,2,0:T(4,128)(2,1)S(1)}, bf16[1,4,64,128]{3,1,2,0:T(4,128)(2,1)S(1)}, u32[]{:S(2)}, u32[]{:S(2)}) collective-permute-start(bf16[1,4,64,128]{3,1,2,0:T(4,128)(2,1)S(1)} %get-tuple-element.13), channel_id=1, source_target_pairs={{1,0},{2,1},{3,2},{4,3},{5,4},{6,5},{7,6},{8,7},{9,8},{10,9},{11,1... | collective-permute-start | bytes 196616 | tf_op jit(solution)/shard_map/ppermute | solution.py:22
  27.3 1.4 %collective-permute-done.5 = bf16[1,4,64,128]{3,1,2,0:T(4,128)(2,1)S(1)} collective-permute-done((bf16[1,4,64,128]{3,1,2,0:T(4,128)(2,1)S(1)}, bf16[1,4,64,128]{3,1,2,0:T(4,128)(2,1)S(1)}, u32[]{:S(2)}, u32[]{:S(2)}) %collective-permute-start.5) | collective-permute-done | bytes 65568 | tf_op jit(solution)/shard_map/ppermute | solution.py:22
  29.3 5.3 %collective-permute-start.6 = (bf16[1,4,64,128]{3,1,2,0:T(4,128)(2,1)S(1)}, bf16[1,4,64,128]{3,1,2,0:T(4,128)(2,1)S(1)}, u32[]{:S(2)}, u32[]{:S(2)}) collective-permute-start(bf16[1,4,64,128]{3,1,2,0:T(4,128)(2,1)S(1)} %get-tuple-element.10), channel_id=1, source_target_pairs={{0,1},{1,2},{2,3},{3,4},{4,5},{5,6},{6,7},{7,8},{8,9},{9,10},{10,1... | collective-permute-start | bytes 196616 | tf_op jit(solution)/shard_map/ppermute | solution.py:19
  34.6 1.3 %collective-permute-start.7 = (bf16[1,4,64,128]{3,1,2,0:T(4,128)(2,1)S(1)}, bf16[1,4,64,128]{3,1,2,0:T(4,128)(2,1)S(1)}, u32[]{:S(2)}, u32[]{:S(2)}) collective-permute-start(bf16[1,4,64,128]{3,1,2,0:T(4,128)(2,1)S(1)} %get-tuple-element.11), channel_id=1, source_target_pairs={{1,0},{2,1},{3,2},{4,3},{5,4},{6,5},{7,6},{8,7},{9,8},{10,9},{11,1... | collective-permute-start | bytes 196616 | tf_op jit(solution)/shard_map/ppermute | solution.py:22
  36.4 1.4 %collective-permute-done.7 = bf16[1,4,64,128]{3,1,2,0:T(4,128)(2,1)S(1)} collective-permute-done((bf16[1,4,64,128]{3,1,2,0:T(4,128)(2,1)S(1)}, bf16[1,4,64,128]{3,1,2,0:T(4,128)(2,1)S(1)}, u32[]{:S(2)}, u32[]{:S(2)}) %collective-permute-start.7) | collective-permute-done | bytes 65568 | tf_op jit(solution)/shard_map/ppermute | solution.py:22
  38.4 0.7 copy.12
  39.1 8.9 %all-to-all-start = ((bf16[2,4,64,128]{3,1,0,2:T(4,128)(2,1)}), bf16[2,4,64,128]{3,1,0,2:T(4,128)(2,1)S(1)}, u32[]{:S(2)}, u32[]{:S(2)}) async-start(bf16[2,4,64,128]{3,1,0,2:T(4,128)(2,1)} %copy.12), calls=%async_computation | async-start | bytes 262144 | tf_op jit(solution)/shard_map/all_to_all | solution.py:77
  48.0 0.6 copy-done.3
  48.6 0.6 dynamic-slice
  49.9 6.0 %all-to-all-done = bf16[2,4,64,128]{3,1,0,2:T(4,128)(2,1)S(1)} async-done(((bf16[2,4,64,128]{3,1,0,2:T(4,128)(2,1)}), bf16[2,4,64,128]{3,1,0,2:T(4,128)(2,1)S(1)}, u32[]{:S(2)}, u32[]{:S(2)}) %all-to-all-start) | async-done | bytes 131104 | tf_op jit(solution)/shard_map/all_to_all | solution.py:77
  56.0 0.6 copy-done.1
  56.8 58.2 %all-reduce.9 = f32[32,32]{1,0:T(8,128)S(1)} all-reduce(f32[32,32]{1,0:T(8,128)S(1)} %convolution_multiply_fusion), channel_id=2, replica_groups=mesh['groups'=2,'dates'=16] {'dates'}, use_global_device_ids=true, to_apply=%region_0.1.clone | all-reduce | flops 1024 | bytes 8192
  114.9 0.6 constant_dynamic-slice_fusion
  (43 shorter events, 5.3 us)
Async XLA Ops:
  0.6 1.0 copy-start
  1.6 0.8 copy-start.2
  3.3 4.5 %collective-permute-start = (bf16[1,4,64,128]{3,1,2,0:T(4,128)(2,1)S(1)}, bf16[1,4,64,128]{3,1,2,0:T(4,128)(2,1)S(1)}, u32[]{:S(2)}, u32[]{:S(2)}) collective-permute-start(bf16[1,4,64,128]{3,1,2,0:T(4,128)(2,1)S(1)} %get-tuple-element.16), channel_id=1, source_target_pairs={{0,1},{1,2},{2,3},{3,4},{4,5},{5,6},{6,7},{7,8},{8,9},{9,10},{10,1... | collective-permute-start | bytes 196616 | tf_op jit(solution)/shard_map/ppermute | solution.py:19
  5.7 5.3 %collective-permute-start.1 = (bf16[1,4,64,128]{3,1,2,0:T(4,128)(2,1)S(1)}, bf16[1,4,64,128]{3,1,2,0:T(4,128)(2,1)S(1)}, u32[]{:S(2)}, u32[]{:S(2)}) collective-permute-start(bf16[1,4,64,128]{3,1,2,0:T(4,128)(2,1)S(1)} %get-tuple-element.17), channel_id=1, source_target_pairs={{1,0},{2,1},{3,2},{4,3},{5,4},{6,5},{7,6},{8,7},{9,8},{10,9},{11,1... | collective-permute-start | bytes 196616 | tf_op jit(solution)/shard_map/ppermute | solution.py:22
  11.7 6.6 %collective-permute-start.2 = (bf16[1,4,64,128]{3,1,2,0:T(4,128)(2,1)S(1)}, bf16[1,4,64,128]{3,1,2,0:T(4,128)(2,1)S(1)}, u32[]{:S(2)}, u32[]{:S(2)}) collective-permute-start(bf16[1,4,64,128]{3,1,2,0:T(4,128)(2,1)S(1)} %get-tuple-element.14), channel_id=1, source_target_pairs={{0,1},{1,2},{2,3},{3,4},{4,5},{5,6},{6,7},{7,8},{8,9},{9,10},{10,1... | collective-permute-start | bytes 196616 | tf_op jit(solution)/shard_map/ppermute | solution.py:19
  16.5 3.1 %collective-permute-start.3 = (bf16[1,4,64,128]{3,1,2,0:T(4,128)(2,1)S(1)}, bf16[1,4,64,128]{3,1,2,0:T(4,128)(2,1)S(1)}, u32[]{:S(2)}, u32[]{:S(2)}) collective-permute-start(bf16[1,4,64,128]{3,1,2,0:T(4,128)(2,1)S(1)} %get-tuple-element.15), channel_id=1, source_target_pairs={{1,0},{2,1},{3,2},{4,3},{5,4},{6,5},{7,6},{8,7},{9,8},{10,9},{11,1... | collective-permute-start | bytes 196616 | tf_op jit(solution)/shard_map/ppermute | solution.py:22
  20.4 6.9 %collective-permute-start.4 = (bf16[1,4,64,128]{3,1,2,0:T(4,128)(2,1)S(1)}, bf16[1,4,64,128]{3,1,2,0:T(4,128)(2,1)S(1)}, u32[]{:S(2)}, u32[]{:S(2)}) collective-permute-start(bf16[1,4,64,128]{3,1,2,0:T(4,128)(2,1)S(1)} %get-tuple-element.12), channel_id=1, source_target_pairs={{0,1},{1,2},{2,3},{3,4},{4,5},{5,6},{6,7},{7,8},{8,9},{9,10},{10,1... | collective-permute-start | bytes 196616 | tf_op jit(solution)/shard_map/ppermute | solution.py:19
  25.5 3.1 %collective-permute-start.5 = (bf16[1,4,64,128]{3,1,2,0:T(4,128)(2,1)S(1)}, bf16[1,4,64,128]{3,1,2,0:T(4,128)(2,1)S(1)}, u32[]{:S(2)}, u32[]{:S(2)}) collective-permute-start(bf16[1,4,64,128]{3,1,2,0:T(4,128)(2,1)S(1)} %get-tuple-element.13), channel_id=1, source_target_pairs={{1,0},{2,1},{3,2},{4,3},{5,4},{6,5},{7,6},{8,7},{9,8},{10,9},{11,1... | collective-permute-start | bytes 196616 | tf_op jit(solution)/shard_map/ppermute | solution.py:22
  29.3 7.0 %collective-permute-start.6 = (bf16[1,4,64,128]{3,1,2,0:T(4,128)(2,1)S(1)}, bf16[1,4,64,128]{3,1,2,0:T(4,128)(2,1)S(1)}, u32[]{:S(2)}, u32[]{:S(2)}) collective-permute-start(bf16[1,4,64,128]{3,1,2,0:T(4,128)(2,1)S(1)} %get-tuple-element.10), channel_id=1, source_target_pairs={{0,1},{1,2},{2,3},{3,4},{4,5},{5,6},{6,7},{7,8},{8,9},{9,10},{10,1... | collective-permute-start | bytes 196616 | tf_op jit(solution)/shard_map/ppermute | solution.py:19
  34.6 3.1 %collective-permute-start.7 = (bf16[1,4,64,128]{3,1,2,0:T(4,128)(2,1)S(1)}, bf16[1,4,64,128]{3,1,2,0:T(4,128)(2,1)S(1)}, u32[]{:S(2)}, u32[]{:S(2)}) collective-permute-start(bf16[1,4,64,128]{3,1,2,0:T(4,128)(2,1)S(1)} %get-tuple-element.11), channel_id=1, source_target_pairs={{1,0},{2,1},{3,2},{4,3},{5,4},{6,5},{7,6},{8,7},{9,8},{10,9},{11,1... | collective-permute-start | bytes 196616 | tf_op jit(solution)/shard_map/ppermute | solution.py:22
  39.1 16.8 %all-to-all-start = ((bf16[2,4,64,128]{3,1,0,2:T(4,128)(2,1)}), bf16[2,4,64,128]{3,1,0,2:T(4,128)(2,1)S(1)}, u32[]{:S(2)}, u32[]{:S(2)}) async-start(bf16[2,4,64,128]{3,1,0,2:T(4,128)(2,1)} %copy.12), calls=%async_computation | async-start | bytes 262144 | tf_op jit(solution)/shard_map/all_to_all | solution.py:77
  48.0 0.7 copy-start.3
  55.9 0.7 copy-start.1
where the time goes:
time: 116 us
  blocking collectives  58.2 us (50%)
  starting transfers between devices  31.7 us (27%)
  waiting for transfers between devices  13.3 us (11%)
  other arithmetic  5.48 us (5%)
  local copies, waits for them, and re-layouts  4.16 us (4%)
  between operations  1.64 us (1%)
    unnamed x1, blocking collectives  58.2 us
    ppermute x4, starting transfers between devices, extended(): lax.ppermute(lax.slice_in_dim(block, block.shape[dim] - width, None, axis...  17.6 us
    all_to_all x1, starting transfers between devices, local(): lax.all_to_all(current.astype(jnp.bfloat16), 'dates', split_axis=2, conca...  8.89 us
    ppermute x4, waiting for transfers between devices, extended(): lax.ppermute(lax.slice_in_dim(block, 0, width, axis=dim), axis, backward)  7.26 us
    all_to_all x1, waiting for transfers between devices, local(): lax.all_to_all(current.astype(jnp.bfloat16), 'dates', split_axis=2, conca...  6.04 us
    ppermute x4, starting transfers between devices, extended(): lax.ppermute(lax.slice_in_dim(block, 0, width, axis=dim), axis, backward)  5.17 us
    unnamed x10, local copies, waits for them, and re-layouts  3.14 us
  transfers between devices with their start and end apart: 9, of which 5 were waited for; matrix products, arithmetic and copies ran while one was open for 2% of the time, Pallas kernels for 0%

commit v1 on v0

v1 whole, which is shorter than its diff:
```python
import functools

import jax
import jax.numpy as jnp
from jax import lax
from jax.experimental import pallas as pl
from jax.experimental.pallas import tpu as pltpu
from jax.sharding import PartitionSpec as P

REGIONS = 8
STEPS = 4
HALO = 8
SHARED = 2

lam_space = 0.2
lam_time = 0.08

LIMIT = 48 * 1024 * 1024


def phi(difference):
    return difference / (1.0 + difference * difference)


class Plan:
    def __init__(self, devices, bands, rows):
        self.devices, self.bands, self.rows = devices, bands, rows
        planes = devices // bands
        self.shared = min(SHARED, planes)
        self.slabs = planes // self.shared
        self.plane_rows = rows // planes
        self.own_rows = rows // devices
        self.slab_rows = rows // self.slabs
        margin = HALO * min(self.slabs - 1, 2)
        self.window = self.slab_rows + margin

    def slab(self, index):
        return index // (self.bands * self.shared)

    def start(self, index):
        first = self.slab(index) * self.slab_rows - HALO
        last = self.rows - self.window
        if isinstance(index, int):
            return min(max(first, 0), last)
        return jnp.clip(first, 0, last)


def anomaly_kernel(plan, scenes_ref, mask_ref, region_ref, send_ref, sums_ref):
    date_dev, bands, rows, cols = scenes_ref.shape
    tiles = rows // 8
    per_region = bands + 1

    def tile_rows(i):
        return pl.ds(pl.multiple_of(i * 8, 8), 8)

    for date in range(date_dev):

        def gather(i, sums):
            clear = mask_ref[date, tile_rows(i)] > 0
            label = jnp.where(clear, region_ref[tile_rows(i)], -1)
            values = [scenes_ref[date, band, tile_rows(i)].astype(jnp.float32) for band in range(bands)]
            out = []
            for g in range(REGIONS):
                here = label == g
                for band in range(bands):
                    out.append(sums[g * per_region + band] + jnp.where(here, values[band], 0.0))
                out.append(sums[g * per_region + bands] + jnp.where(here, 1.0, 0.0))
            return tuple(out)

        zero = jnp.zeros((8, cols), jnp.float32)
        sums = lax.fori_loop(0, tiles, gather, (zero,) * (REGIONS * per_region), unroll=min(tiles, 8))
        for i, total in enumerate(sums):
            sums_ref[date, i : i + 1] = jnp.sum(total, axis=0, keepdims=True)

    means = []
    for date in range(date_dev):
        totals = jnp.sum(sums_ref[date], axis=1, keepdims=True)
        for band in range(bands):
            means.append(
                [
                    totals[g * per_region + band : g * per_region + band + 1]
                    / (totals[g * per_region + bands : g * per_region + bands + 1] + 1.0)
                    for g in range(REGIONS)
                ]
            )

    region = region_ref[...]
    for date in range(date_dev):
        clear = mask_ref[date].astype(jnp.float32)
        for band in range(bands):
            mean = jnp.zeros((rows, cols), jnp.float32)
            for g in range(REGIONS):
                mean = jnp.where(region == g, jnp.broadcast_to(means[date * bands + band][g], (rows, cols)), mean)
            anomaly = (clear * (scenes_ref[date, band].astype(jnp.float32) - mean)).astype(jnp.bfloat16)
            for target in range(band, plan.devices, bands):
                first = plan.start(target)
                send_ref[target, date] = anomaly[first : first + plan.window]


def diffuse_kernel(plan, dates, got_ref, region_ref, stay_ref, send_ref, gram_ref, field_ref):
    window, cols = plan.window, got_ref.shape[-1]
    me = lax.axis_index("dates")
    start = plan.start(me)
    land = (region_ref[pl.ds(pl.multiple_of(start, 8), window)] > 0).astype(jnp.float32)
    row = lax.broadcasted_iota(jnp.int32, (window, cols), 0)
    col = lax.broadcasted_iota(jnp.int32, (window, cols), 1)
    down = jnp.where(row < window - 1, pltpu.roll(land, window - 1, 0), 0.0)
    right = jnp.where(col < cols - 1, pltpu.roll(land, cols - 1, 1), 0.0)
    row_weight = lam_space * land * down
    col_weight = lam_space * land * right

    def at(t):
        return pl.ds(pl.multiple_of(t * window, 8), window)

    def load_first(t):
        return got_ref[t].astype(jnp.float32)

    def load(t):
        return field_ref[at(t)]

    for step in range(STEPS):
        read = load_first if step == 0 else load

        def advance(current, following, date_in):
            row_flux = row_weight * phi(pltpu.roll(current, window - 1, 0) - current)
            col_flux = col_weight * phi(pltpu.roll(current, cols - 1, 1) - current)
            date_out = jnp.zeros_like(current) if following is None else lam_time * phi(following - current)
            new = (
                current
                + (row_flux - pltpu.roll(row_flux, 1, 0))
                + (col_flux - pltpu.roll(col_flux, 1, 1))
                + (date_out - date_in)
            )
            return new, date_out

        def one(t, carry):
            current, date_in = carry
            following = read(t + 1)
            new, date_out = advance(current, following, date_in)
            field_ref[at(t)] = new
            return following, date_out

        last, date_in = lax.fori_loop(
            0, dates - 1, one, (read(0), jnp.zeros((window, cols), jnp.float32)), unroll=1
        )
        new, _ = advance(last, None, date_in)
        field_ref[at(dates - 1)] = new

    half = plan.plane_rows // 2
    pair = (me // 2) % 2
    plane_first = (me // plan.bands) * plan.plane_rows - start
    stay_first = pl.multiple_of(plane_first + pair * half, 8)
    send_first = pl.multiple_of(plane_first + (1 - pair) * half, 8)
    for t in range(dates):
        stay_ref[t] = field_ref[pl.ds(t * window + stay_first, half)].astype(jnp.bfloat16)
        send_ref[t] = field_ref[pl.ds(t * window + send_first, half)].astype(jnp.bfloat16)

    slab_first = plan.slab(me) * plan.slab_rows - start

    def gram(i, total):
        rows = jnp.concatenate(
            [field_ref[pl.ds(slab_first + 2 * i + j, dates, stride=window)] for j in range(2)], axis=1
        ).astype(jnp.bfloat16)
        return total + lax.dot_general(
            rows, rows, (((1,), (1,)), ((), ())), preferred_element_type=jnp.float32
        )

    gram_ref[...] = lax.fori_loop(
        0, plan.slab_rows // 2, gram, jnp.zeros((dates, dates), jnp.float32), unroll=min(8, plan.slab_rows // 2)
    )


def swap(x, bit):
    count = lax.axis_size("dates")
    return lax.ppermute(x, "dates", [(i, i ^ bit) for i in range(count)])


def local(scenes, cloud_mask, region):
    date_dev, bands, rows, cols = scenes.shape
    devices = lax.axis_size("dates")
    dates = date_dev * devices
    plan = Plan(devices, bands, rows)
    me = lax.axis_index("dates")
    vmem = pl.BlockSpec(memory_space=pltpu.VMEM)
    params = pltpu.CompilerParams(vmem_limit_bytes=LIMIT)

    send = pl.pallas_call(
        functools.partial(anomaly_kernel, plan),
        out_shape=jax.ShapeDtypeStruct((devices, date_dev, plan.window, cols), jnp.bfloat16),
        in_specs=[vmem] * 3,
        out_specs=vmem,
        scratch_shapes=[pltpu.VMEM((date_dev, REGIONS * (bands + 1), cols), jnp.float32)],
        compiler_params=params,
    )(scenes, cloud_mask, region)
    got = lax.all_to_all(send, "dates", split_axis=0, concat_axis=0, tiled=True)
    half = plan.plane_rows // 2
    stay, away, gram = pl.pallas_call(
        functools.partial(diffuse_kernel, plan, dates),
        out_shape=(
            jax.ShapeDtypeStruct((dates, half, cols), jnp.bfloat16),
            jax.ShapeDtypeStruct((dates, half, cols), jnp.bfloat16),
            jax.ShapeDtypeStruct((dates, dates), jnp.float32),
        ),
        in_specs=[vmem] * 2,
        out_specs=(vmem,) * 3,
        scratch_shapes=[pltpu.VMEM((dates * plan.window, cols), jnp.float32)],
        compiler_params=params,
    )(got.reshape(dates, plan.window, cols), region)

    own = plan.own_rows
    core, pair = me % 2, (me // 2) % 2
    other = swap(away, 2)
    gram = gram + swap(gram, 2)
    both = jnp.stack([jnp.where(pair == 0, stay, other), jnp.where(pair == 0, other, stay)], axis=1)
    low, high = both[:, :, :own], both[:, :, own:]
    mine = jnp.where(core == 0, low, high)
    theirs = swap(jnp.where(core == 0, high, low), 1)
    gram = gram + swap(gram, 1)
    smoothed = jnp.stack(
        [jnp.where(core == 0, mine, theirs), jnp.where(core == 0, theirs, mine)], axis=2
    ).reshape(dates, bands, own, cols)
    bit = bands * plan.shared
    while bit < devices:
        gram = gram + swap(gram, bit)
        bit *= 2
    similarity = lax.dynamic_slice_in_dim(gram, me * date_dev, date_dev, 0) / (bands * rows * cols)
    return smoothed, similarity


def solution(mesh):
    in_specs = (
        P(("groups", "dates"), None, None, None),
        P(("groups", "dates"), None, None),
        P("groups", None),
    )
    out_specs = (P("groups", None, "dates", None), P(("groups", "dates"), None))
    return jax.shard_map(local, mesh=mesh, in_specs=in_specs, out_specs=out_specs, check_vma=False)
```

time: 116 us -> 54.1 us (0.47)
  blocking collectives: 58.2 us -> 18.3 us
  starting transfers between devices: 31.7 us -> 3.53 us
  Pallas kernels: 0 us -> 20.5 us
  waiting for transfers between devices: 13.3 us -> 6.67 us
  other arithmetic: 5.48 us -> 0.81 us
    unnamed x1 -> x0, blocking collectives: 58.2 us -> none
    pallas_call x0 -> x2, Pallas kernels: none -> 20.5 us  [the longest x1 20 us: local(): pl.pallas_call(functools.partial(diffuse_kernel, plan, dates), out_shape=...]
    ppermute x8 -> x5, starting transfers between devices: 22.8 us -> 3.53 us  [swap(): return lax.ppermute(x, 'dates', [(i, i ^ bit) for i in range(count)])]
    all_to_all x0 -> x1, blocking collectives: none -> 18.3 us  [local(): got = lax.all_to_all(send, 'dates', split_axis=0, concat_axis=0, tiled=True)]
    all_to_all x1 -> x0, starting transfers between devices: 8.89 us -> none  [local(): lax.all_to_all(current.astype(jnp.bfloat16), 'dates', split_axis=2, conca...]
    all_to_all x1 -> x0, waiting for transfers between devices: 6.04 us -> none  [local(): lax.all_to_all(current.astype(jnp.bfloat16), 'dates', split_axis=2, conca...]
    mul x16 -> x0, other arithmetic: 2.74 us -> none  [the longest x5 1.49 us: advance(): lam_space * col_weight]
    convert_element_type x9 -> x0, other arithmetic: 2.65 us -> none  [the longest x4 1.04 us: local(): current.astype(jnp.bfloat16)]
  transfers between devices with their start and end apart: 9 -> 5, of which waited for: 5 -> 3; matrix products, arithmetic and copies ran while one was open for 2% -> 1% of each run, Pallas kernels for 0% -> 0%
where the time goes in v1:
time: 54.1 us; the launch traced here: 53.8 us
  Pallas kernels  20.5 us (38%)
  blocking collectives  18.3 us (34%)
  waiting for transfers between devices  6.67 us (12%)
  starting transfers between devices  3.53 us (7%)
  local copies, waits for them, and re-layouts  3.24 us (6%)
  other arithmetic  0.81 us (1%)
  between operations  0.75 us (1%)
    pallas_call x1, Pallas kernels, local(): pl.pallas_call(functools.partial(diffuse_kernel, plan, dates), out_shape=...  20 us
    all_to_all x1, blocking collectives, local(): got = lax.all_to_all(send, 'dates', split_axis=0, concat_axis=0, tiled=True)  18.3 us
    ppermute x5, waiting for transfers between devices, swap(): return lax.ppermute(x, 'dates', [(i, i ^ bit) for i in range(count)])  6.67 us
    ppermute x5, starting transfers between devices, swap(): return lax.ppermute(x, 'dates', [(i, i ^ bit) for i in range(count)])  3.53 us
    unnamed x9, local copies, waits for them, and re-layouts  3.22 us
  transfers between devices with their start and end apart: 5, of which 3 were waited for; matrix products, arithmetic and copies ran while one was open for 1% of the time, Pallas kernels for 0%

profile of v1, /device:TPU:0, one launch (start us, length us, event | category | flops | bytes accessed | tf_op | source)
XLA Modules:
  0.0 53.8 jit_solution(12276931359471463771)
XLA Ops:
  0.6 0.0 copy-start
  0.6 0.9 %copy-done = bf16[2,4,64,128]{3,2,1,0:T(8,128)(2,1)S(1)} copy-done((bf16[2,4,64,128]{3,2,1,0:T(8,128)(2,1)S(1)}, bf16[2,4,64,128]{3,2,1,0:T(8,128)(2,1)}, u32[]{:S(2)}) %copy-start) | copy-done | bytes 131096
  1.5 0.0 copy-start.1
  1.5 0.8 %copy-done.1 = s32[64,128]{1,0:T(8,128)S(1)} copy-done((s32[64,128]{1,0:T(8,128)S(1)}, s32[64,128]{1,0:T(8,128)}, u32[]{:S(2)}) %copy-start.1) | copy-done | bytes 32792
  2.3 0.8 %copy-done.3 = s32[2,64,128]{2,1,0:T(8,128)S(1)} copy-done((s32[2,64,128]{2,1,0:T(8,128)S(1)}, s32[2,64,128]{2,1,0:T(8,128)}, u32[]{:S(2)}) %copy-start.3) | copy-done | bytes 65560
  3.1 0.5 shard_map.50
  3.6 0.0 copy-start.2
  3.7 18.3 %all_to_all.5 = bf16[16,2,40,128]{3,2,1,0:T(8,128)(2,1)S(1)} all-to-all(bf16[16,2,40,128]{3,2,1,0:T(8,128)(2,1)S(1)} %shard_map.50), channel_id=1, replica_groups=mesh['groups'=2,'dates'=16] {'dates'}, dimensions={0} | all-to-all | bytes 655360 | tf_op jit(solution)/shard_map/all_to_all | solution.py:195
  21.9 0.0 copy-done.2
  21.9 20.0 %shard_map.51 = (bf16[32,8,128]{2,1,0:T(8,128)(2,1)S(1)}, bf16[32,8,128]{2,1,0:T(8,128)(2,1)S(1)}, f32[32,32]{1,0:T(8,128)S(1)}) custom-call(bf16[32,40,128]{2,1,0:T(8,128)(2,1)S(1)} %bitcast.10, s32[64,128]{1,0:T(8,128)S(1)} %copy-done.2), custom_call_target="tpu_custom_call" | custom-call | tf_op jit(solution)/shard_map/pallas_call | solution.py:197
  41.9 0.1 collective-permute-start
  42.0 2.0 %collective-permute-start.2 = (f32[32,32]{1,0:T(8,128)S(1)}, f32[32,32]{1,0:T(8,128)S(1)}, u32[]{:S(2)}, u32[]{:S(2)}) collective-permute-start(f32[32,32]{1,0:T(8,128)S(1)} %get-tuple-element.7), channel_id=1, source_target_pairs={{0,2},{1,3},{2,0},{3,1},{4,6},{5,7},{6,4},{7,5},{8,10},{9,11},{10,... | collective-permute-start | bytes 12296 | tf_op jit(solution)/shard_map/ppermute | solution.py:175
  44.0 2.4 %collective-permute-done.2 = f32[32,32]{1,0:T(8,128)S(1)} collective-permute-done((f32[32,32]{1,0:T(8,128)S(1)}, f32[32,32]{1,0:T(8,128)S(1)}, u32[]{:S(2)}, u32[]{:S(2)}) %collective-permute-start.2) | collective-permute-done | bytes 4128 | tf_op jit(solution)/shard_map/ppermute | solution.py:175
  46.4 0.0 collective-permute-start.3
  46.5 1.1 %collective-permute-done.3 = f32[32,32]{1,0:T(8,128)S(1)} collective-permute-done((f32[32,32]{1,0:T(8,128)S(1)}, f32[32,32]{1,0:T(8,128)S(1)}, u32[]{:S(2)}, u32[]{:S(2)}) %collective-permute-start.3) | collective-permute-done | bytes 4128 | tf_op jit(solution)/shard_map/ppermute | solution.py:175
  47.6 1.4 %collective-permute-start.4 = (f32[32,32]{1,0:T(8,128)S(1)}, f32[32,32]{1,0:T(8,128)S(1)}, u32[]{:S(2)}, u32[]{:S(2)}) collective-permute-start(f32[32,32]{1,0:T(8,128)S(1)} %add.23), channel_id=1, source_target_pairs={{0,8},{1,9},{2,10},{3,11},{4,12},{5,13},{6,14},{7,15},{8,0},{9,1},... | collective-permute-start | bytes 12296 | tf_op jit(solution)/shard_map/ppermute | solution.py:175
  49.0 0.0 collective-permute-done
  49.1 0.1 collective-permute-start.1
  49.2 3.1 %collective-permute-done.4 = f32[32,32]{1,0:T(8,128)S(1)} collective-permute-done((f32[32,32]{1,0:T(8,128)S(1)}, f32[32,32]{1,0:T(8,128)S(1)}, u32[]{:S(2)}, u32[]{:S(2)}) %collective-permute-start.4) | collective-permute-done | bytes 4128 | tf_op jit(solution)/shard_map/ppermute | solution.py:175
  52.3 0.6 %fusion.1 = f32[2,32]{1,0:T(2,128)} fusion(f32[32,32]{1,0:T(8,128)S(1)} %collective-permute-done.4, s32[]{:T(128)S(6)} %select_n.61, f32[32,32]{1,0:T(8,128)S(1)} %add.23), kind=kLoop, calls=%fused_computation.12 | loop fusion | flops 128 | bytes 772 | tf_op jit(solution)/shard_map/div | solution.py:226
  52.8 0.0 collective-permute-done.1
  52.8 0.1 select_bitcast_fusion.1
  52.9 0.1 pad_maximum_fusion
  53.0 0.7 %copy.6 = bf16[32,4,4,128]{3,2,1,0:T(4,128)(2,1)} copy(bf16[32,4,4,128]{3,0,2,1:T(8,128)(2,1)S(1)} %bitcast.11) | data formatting | bytes 262144
  (6 shorter events, 0.1 us)
Async XLA Ops:
  0.6 0.9 %copy-start = (bf16[2,4,64,128]{3,2,1,0:T(8,128)(2,1)S(1)}, bf16[2,4,64,128]{3,2,1,0:T(8,128)(2,1)}, u32[]{:S(2)}) copy-start(bf16[2,4,64,128]{3,2,1,0:T(8,128)(2,1)} %scenes_ref.1) | copy-start | bytes 393220
  1.5 0.8 %copy-start.1 = (s32[64,128]{1,0:T(8,128)S(1)}, s32[64,128]{1,0:T(8,128)}, u32[]{:S(2)}) copy-start(s32[64,128]{1,0:T(8,128)} %region_ref.3) | copy-start | bytes 98308
  2.3 0.8 %copy-start.3 = (s32[2,64,128]{2,1,0:T(8,128)S(1)}, s32[2,64,128]{2,1,0:T(8,128)}, u32[]{:S(2)}) copy-start(s32[2,64,128]{2,1,0:T(8,128)} %mask_ref.1) | copy-start | bytes 196612
  3.6 18.3 %copy-start.2 = (s32[64,128]{1,0:T(8,128)S(1)}, s32[64,128]{1,0:T(8,128)}, u32[]{:S(2)}) copy-start(s32[64,128]{1,0:T(8,128)} %region_ref.3) | copy-start | bytes 98308
  41.9 7.1 %collective-permute-start = (bf16[32,8,128]{2,1,0:T(8,128)(2,1)S(1)}, bf16[32,8,128]{2,1,0:T(8,128)(2,1)S(1)}, u32[]{:S(2)}, u32[]{:S(2)}) collective-permute-start(bf16[32,8,128]{2,1,0:T(8,128)(2,1)S(1)} %get-tuple-element.6), channel_id=1, source_target_pairs={{0,2},{1,3},{2,0},{3,1},{4,6},{5,7},{6,4},{7,5},{8,10},{9,11},{10,... | collective-permute-start | bytes 196616 | tf_op jit(solution)/shard_map/ppermute | solution.py:175
  42.0 4.4 %collective-permute-start.2 = (f32[32,32]{1,0:T(8,128)S(1)}, f32[32,32]{1,0:T(8,128)S(1)}, u32[]{:S(2)}, u32[]{:S(2)}) collective-permute-start(f32[32,32]{1,0:T(8,128)S(1)} %get-tuple-element.7), channel_id=1, source_target_pairs={{0,2},{1,3},{2,0},{3,1},{4,6},{5,7},{6,4},{7,5},{8,10},{9,11},{10,... | collective-permute-start | bytes 12296 | tf_op jit(solution)/shard_map/ppermute | solution.py:175
  46.4 1.2 %collective-permute-start.3 = (f32[32,32]{1,0:T(8,128)S(1)}, f32[32,32]{1,0:T(8,128)S(1)}, u32[]{:S(2)}, u32[]{:S(2)}) collective-permute-start(f32[32,32]{1,0:T(8,128)S(1)} %add.22), channel_id=1, source_target_pairs={{0,1},{1,0},{2,3},{3,2},{4,5},{5,4},{6,7},{7,6},{8,9},{9,8},{10,11... | collective-permute-start | bytes 12296 | tf_op jit(solution)/shard_map/ppermute | solution.py:175
  47.6 4.6 %collective-permute-start.4 = (f32[32,32]{1,0:T(8,128)S(1)}, f32[32,32]{1,0:T(8,128)S(1)}, u32[]{:S(2)}, u32[]{:S(2)}) collective-permute-start(f32[32,32]{1,0:T(8,128)S(1)} %add.23), channel_id=1, source_target_pairs={{0,8},{1,9},{2,10},{3,11},{4,12},{5,13},{6,14},{7,15},{8,0},{9,1},... | collective-permute-start | bytes 12296 | tf_op jit(solution)/shard_map/ppermute | solution.py:175
  49.1 3.7 %collective-permute-start.1 = (bf16[32,2,4,128]{3,2,0,1:T(4,128)(2,1)S(1)}, bf16[32,2,4,128]{3,2,0,1:T(4,128)(2,1)S(1)}, u32[]{:S(2)}, u32[]{:S(2)}) collective-permute-start(bf16[32,2,4,128]{3,2,0,1:T(4,128)(2,1)S(1)} %broadcast_select_fusion), channel_id=1, source_target_pairs={{0,1},{1,0},{2,3},{3,2},{4,5},{5,4},{6,7},{7,6},{8,9},{9,8},{10,11... | collective-permute-start | bytes 196616 | tf_op jit(solution)/shard_map/ppermute | solution.py:175

commit v2 on v1

--- a/solution.py
+++ b/solution.py
@@ -11,6 +11,9 @@
 STEPS = 4
 HALO = 8
 SHARED = 2
+
+CHUNK = 4
+UNROLL = 7
 
 lam_space = 0.2
 lam_time = 0.08
@@ -106,45 +109,45 @@
     col = lax.broadcasted_iota(jnp.int32, (window, cols), 1)
     down = jnp.where(row < window - 1, pltpu.roll(land, window - 1, 0), 0.0)
     right = jnp.where(col < cols - 1, pltpu.roll(land, cols - 1, 1), 0.0)
-    row_weight = lam_space * land * down
-    col_weight = lam_space * land * right
-
-    def at(t):
-        return pl.ds(pl.multiple_of(t * window, 8), window)
-
-    def load_first(t):
-        return got_ref[t].astype(jnp.float32)
-
-    def load(t):
-        return field_ref[at(t)]
+    row_weight = jnp.concatenate([lam_space * land * down] * CHUNK, axis=0)
+    col_weight = jnp.concatenate([lam_space * land * right] * CHUNK, axis=0)
+    source = lax.broadcasted_iota(jnp.int32, (cols, cols), 0)
+    target = lax.broadcasted_iota(jnp.int32, (cols, cols), 1)
+    same = (source == target).astype(jnp.float32)
+    onward = ((source == target + 1).astype(jnp.float32) - same).astype(jnp.bfloat16)
+    inflow = (same - (source + 1 == target).astype(jnp.float32)).astype(jnp.bfloat16)
+    length, chunks = CHUNK * window, dates // CHUNK
 
     for step in range(STEPS):
-        read = load_first if step == 0 else load
+
+        def read(t):
+            ref = got_ref if step == 0 else field_ref
+            return ref[pl.ds(pl.multiple_of(t * window, 8), length)].astype(jnp.float32)
 
         def advance(current, following, date_in):
-            row_flux = row_weight * phi(pltpu.roll(current, window - 1, 0) - current)
-            col_flux = col_weight * phi(pltpu.roll(current, cols - 1, 1) - current)
-            date_out = jnp.zeros_like(current) if following is None else lam_time * phi(following - current)
+            difference = jnp.dot(current.astype(jnp.bfloat16), onward, preferred_element_type=jnp.float32)
+            col_flux = (col_weight * phi(difference)).astype(jnp.bfloat16)
+            row_flux = row_weight * phi(pltpu.roll(current, length - 1, 0) - current)
+            date_flux = lam_time * phi(following - current)
             new = (
                 current
                 + (row_flux - pltpu.roll(row_flux, 1, 0))
-                + (col_flux - pltpu.roll(col_flux, 1, 1))
-                + (date_out - date_in)
+                + jnp.dot(col_flux, inflow, preferred_element_type=jnp.float32)
+                + (date_flux - jnp.concatenate([date_in, date_flux[:-window]], axis=0))
             )
-            return new, date_out
-
-        def one(t, carry):
-            current, date_in = carry
-            following = read(t + 1)
-            new, date_out = advance(current, following, date_in)
-            field_ref[at(t)] = new
-            return following, date_out
-
-        last, date_in = lax.fori_loop(
-            0, dates - 1, one, (read(0), jnp.zeros((window, cols), jnp.float32)), unroll=1
+            return new, date_flux[-window:]
+
+        def one(k, date_in):
+            new, date_out = advance(read(k * CHUNK), read(k * CHUNK + 1), date_in)
+            field_ref[pl.ds(pl.multiple_of(k * length, 8), length)] = new
+            return date_out
+
+        date_in = lax.fori_loop(
+            0, chunks - 1, one, jnp.zeros((window, cols), jnp.float32), unroll=min(chunks - 1, UNROLL)
         )
-        new, _ = advance(last, None, date_in)
-        field_ref[at(dates - 1)] = new
+        current = read((chunks - 1) * CHUNK)
+        new, _ = advance(current, jnp.concatenate([current[window:], current[-window:]], axis=0), date_in)
+        field_ref[pl.ds((chunks - 1) * length, length)] = new
 
     half = plan.plane_rows // 2
     pair = (me // 2) % 2
@@ -205,7 +208,7 @@
         out_specs=(vmem,) * 3,
         scratch_shapes=[pltpu.VMEM((dates * plan.window, cols), jnp.float32)],
         compiler_params=params,
-    )(got.reshape(dates, plan.window, cols), region)
+    )(got.reshape(dates * plan.window, cols), region)
 
     own = plan.own_rows
     core, pair = me % 2, (me // 2) % 2

time: 54.1 us -> 37.1 us (0.69)
  Pallas kernels: 20.5 us -> 3.47 us
    pallas_call x1, Pallas kernels: 20 us -> 2.97 us  [local(): pl.pallas_call(functools.partial(diffuse_kernel, plan, dates), out_shape=...]
  transfers between devices with their start and end apart: 5 -> 5, of which waited for: 3 -> 3; matrix products, arithmetic and copies ran while one was open for 1% -> 2% of each run, Pallas kernels for 0% -> 0%
where the time goes in v2:
time: 37.1 us; the launch traced here: 36.8 us
  blocking collectives  18.3 us (49%)
  waiting for transfers between devices  6.67 us (18%)
  starting transfers between devices  3.53 us (10%)
  Pallas kernels  3.47 us (9%)
  local copies, waits for them, and re-layouts  3.24 us (9%)
  other arithmetic  0.81 us (2%)
  between operations  0.75 us (2%)
    all_to_all x1, blocking collectives, local(): got = lax.all_to_all(send, 'dates', split_axis=0, concat_axis=0, tiled=True)  18.3 us
    ppermute x5, waiting for transfers between devices, swap(): return lax.ppermute(x, 'dates', [(i, i ^ bit) for i in range(count)])  6.67 us
    ppermute x5, starting transfers between devices, swap(): return lax.ppermute(x, 'dates', [(i, i ^ bit) for i in range(count)])  3.53 us
    unnamed x9, local copies, waits for them, and re-layouts  3.22 us
    pallas_call x1, Pallas kernels, local(): pl.pallas_call(functools.partial(diffuse_kernel, plan, dates), out_shape=...  2.97 us
  transfers between devices with their start and end apart: 5, of which 3 were waited for; matrix products, arithmetic and copies ran while one was open for 2% of the time, Pallas kernels for 0%

profile of v2, /device:TPU:0, one launch (start us, length us, event | category | flops | bytes accessed | tf_op | source)
XLA Modules:
  0.0 36.8 jit_solution(18404355937076425498)
XLA Ops:
  0.6 0.0 copy-start
  0.6 0.9 %copy-done = bf16[2,4,64,128]{3,2,1,0:T(8,128)(2,1)S(1)} copy-done((bf16[2,4,64,128]{3,2,1,0:T(8,128)(2,1)S(1)}, bf16[2,4,64,128]{3,2,1,0:T(8,128)(2,1)}, u32[]{:S(2)}) %copy-start) | copy-done | bytes 131096
  1.5 0.0 copy-start.1
  1.5 0.8 %copy-done.1 = s32[64,128]{1,0:T(8,128)S(1)} copy-done((s32[64,128]{1,0:T(8,128)S(1)}, s32[64,128]{1,0:T(8,128)}, u32[]{:S(2)}) %copy-start.1) | copy-done | bytes 32792
  2.3 0.8 %copy-done.3 = s32[2,64,128]{2,1,0:T(8,128)S(1)} copy-done((s32[2,64,128]{2,1,0:T(8,128)S(1)}, s32[2,64,128]{2,1,0:T(8,128)}, u32[]{:S(2)}) %copy-start.3) | copy-done | bytes 65560
  3.1 0.5 %shard_map.50 = bf16[16,2,40,128]{3,2,1,0:T(8,128)(2,1)S(1)} custom-call(bf16[2,4,64,128]{3,2,1,0:T(8,128)(2,1)S(1)} %copy-done, s32[2,64,128]{2,1,0:T(8,128)S(1)} %copy-done.3, s32[64,128]{1,0:T(8,128)S(1)} %copy-done.1), custom_call_target="tpu_custom_call" | custom-call | tf_op jit(solution)/shard_map/pallas_call | solution.py:190
  3.6 0.0 copy-start.2
  3.7 18.3 %all_to_all.5 = bf16[16,2,40,128]{3,2,1,0:T(8,128)(2,1)S(1)} all-to-all(bf16[16,2,40,128]{3,2,1,0:T(8,128)(2,1)S(1)} %shard_map.50), channel_id=1, replica_groups=mesh['groups'=2,'dates'=16] {'dates'}, dimensions={0} | all-to-all | bytes 655360 | tf_op jit(solution)/shard_map/all_to_all | solution.py:198
  21.9 0.0 copy-done.2
  21.9 3.0 %shard_map.51 = (bf16[32,8,128]{2,1,0:T(8,128)(2,1)S(1)}, bf16[32,8,128]{2,1,0:T(8,128)(2,1)S(1)}, f32[32,32]{1,0:T(8,128)S(1)}) custom-call(bf16[1280,128]{1,0:T(8,128)(2,1)S(1)} %bitcast.10, s32[64,128]{1,0:T(8,128)S(1)} %copy-done.2), custom_call_target="tpu_custom_call" | custom-call | tf_op jit(solution)/shard_map/pallas_call | solution.py:200
  24.9 0.1 collective-permute-start
  25.0 2.0 %collective-permute-start.2 = (f32[32,32]{1,0:T(8,128)S(1)}, f32[32,32]{1,0:T(8,128)S(1)}, u32[]{:S(2)}, u32[]{:S(2)}) collective-permute-start(f32[32,32]{1,0:T(8,128)S(1)} %get-tuple-element.7), channel_id=1, source_target_pairs={{0,2},{1,3},{2,0},{3,1},{4,6},{5,7},{6,4},{7,5},{8,10},{9,11},{10,... | collective-permute-start | bytes 12296 | tf_op jit(solution)/shard_map/ppermute | solution.py:178
  27.0 2.4 %collective-permute-done.2 = f32[32,32]{1,0:T(8,128)S(1)} collective-permute-done((f32[32,32]{1,0:T(8,128)S(1)}, f32[32,32]{1,0:T(8,128)S(1)}, u32[]{:S(2)}, u32[]{:S(2)}) %collective-permute-start.2) | collective-permute-done | bytes 4128 | tf_op jit(solution)/shard_map/ppermute | solution.py:178
  29.4 0.0 collective-permute-start.3
  29.5 1.1 %collective-permute-done.3 = f32[32,32]{1,0:T(8,128)S(1)} collective-permute-done((f32[32,32]{1,0:T(8,128)S(1)}, f32[32,32]{1,0:T(8,128)S(1)}, u32[]{:S(2)}, u32[]{:S(2)}) %collective-permute-start.3) | collective-permute-done | bytes 4128 | tf_op jit(solution)/shard_map/ppermute | solution.py:178
  30.6 1.4 %collective-permute-start.4 = (f32[32,32]{1,0:T(8,128)S(1)}, f32[32,32]{1,0:T(8,128)S(1)}, u32[]{:S(2)}, u32[]{:S(2)}) collective-permute-start(f32[32,32]{1,0:T(8,128)S(1)} %add.23), channel_id=1, source_target_pairs={{0,8},{1,9},{2,10},{3,11},{4,12},{5,13},{6,14},{7,15},{8,0},{9,1},... | collective-permute-start | bytes 12296 | tf_op jit(solution)/shard_map/ppermute | solution.py:178
  32.0 0.0 collective-permute-done
  32.1 0.1 collective-permute-start.1
  32.2 3.1 %collective-permute-done.4 = f32[32,32]{1,0:T(8,128)S(1)} collective-permute-done((f32[32,32]{1,0:T(8,128)S(1)}, f32[32,32]{1,0:T(8,128)S(1)}, u32[]{:S(2)}, u32[]{:S(2)}) %collective-permute-start.4) | collective-permute-done | bytes 4128 | tf_op jit(solution)/shard_map/ppermute | solution.py:178
  35.3 0.6 %fusion.1 = f32[2,32]{1,0:T(2,128)} fusion(f32[32,32]{1,0:T(8,128)S(1)} %collective-permute-done.4, s32[]{:T(128)S(6)} %select_n.61, f32[32,32]{1,0:T(8,128)S(1)} %add.23), kind=kLoop, calls=%fused_computation.12 | loop fusion | flops 128 | bytes 772 | tf_op jit(solution)/shard_map/div | solution.py:229
  35.8 0.0 collective-permute-done.1
  35.8 0.1 select_bitcast_fusion.1
  35.9 0.1 pad_maximum_fusion
  36.0 0.7 %copy.6 = bf16[32,4,4,128]{3,2,1,0:T(4,128)(2,1)} copy(bf16[32,4,4,128]{3,0,2,1:T(8,128)(2,1)S(1)} %bitcast.11) | data formatting | bytes 262144
  (6 shorter events, 0.1 us)
Async XLA Ops:
  0.6 0.9 %copy-start = (bf16[2,4,64,128]{3,2,1,0:T(8,128)(2,1)S(1)}, bf16[2,4,64,128]{3,2,1,0:T(8,128)(2,1)}, u32[]{:S(2)}) copy-start(bf16[2,4,64,128]{3,2,1,0:T(8,128)(2,1)} %scenes_ref.1) | copy-start | bytes 393220
  1.5 0.8 %copy-start.1 = (s32[64,128]{1,0:T(8,128)S(1)}, s32[64,128]{1,0:T(8,128)}, u32[]{:S(2)}) copy-start(s32[64,128]{1,0:T(8,128)} %region_ref.3) | copy-start | bytes 98308
  2.3 0.8 %copy-start.3 = (s32[2,64,128]{2,1,0:T(8,128)S(1)}, s32[2,64,128]{2,1,0:T(8,128)}, u32[]{:S(2)}) copy-start(s32[2,64,128]{2,1,0:T(8,128)} %mask_ref.1) | copy-start | bytes 196612
  3.6 18.3 %copy-start.2 = (s32[64,128]{1,0:T(8,128)S(1)}, s32[64,128]{1,0:T(8,128)}, u32[]{:S(2)}) copy-start(s32[64,128]{1,0:T(8,128)} %region_ref.3) | copy-start | bytes 98308
  24.9 7.1 %collective-permute-start = (bf16[32,8,128]{2,1,0:T(8,128)(2,1)S(1)}, bf16[32,8,128]{2,1,0:T(8,128)(2,1)S(1)}, u32[]{:S(2)}, u32[]{:S(2)}) collective-permute-start(bf16[32,8,128]{2,1,0:T(8,128)(2,1)S(1)} %get-tuple-element.6), channel_id=1, source_target_pairs={{0,2},{1,3},{2,0},{3,1},{4,6},{5,7},{6,4},{7,5},{8,10},{9,11},{10,... | collective-permute-start | bytes 196616 | tf_op jit(solution)/shard_map/ppermute | solution.py:178
  25.0 4.4 %collective-permute-start.2 = (f32[32,32]{1,0:T(8,128)S(1)}, f32[32,32]{1,0:T(8,128)S(1)}, u32[]{:S(2)}, u32[]{:S(2)}) collective-permute-start(f32[32,32]{1,0:T(8,128)S(1)} %get-tuple-element.7), channel_id=1, source_target_pairs={{0,2},{1,3},{2,0},{3,1},{4,6},{5,7},{6,4},{7,5},{8,10},{9,11},{10,... | collective-permute-start | bytes 12296 | tf_op jit(solution)/shard_map/ppermute | solution.py:178
  29.4 1.2 %collective-permute-start.3 = (f32[32,32]{1,0:T(8,128)S(1)}, f32[32,32]{1,0:T(8,128)S(1)}, u32[]{:S(2)}, u32[]{:S(2)}) collective-permute-start(f32[32,32]{1,0:T(8,128)S(1)} %add.22), channel_id=1, source_target_pairs={{0,1},{1,0},{2,3},{3,2},{4,5},{5,4},{6,7},{7,6},{8,9},{9,8},{10,11... | collective-permute-start | bytes 12296 | tf_op jit(solution)/shard_map/ppermute | solution.py:178
  30.6 4.6 %collective-permute-start.4 = (f32[32,32]{1,0:T(8,128)S(1)}, f32[32,32]{1,0:T(8,128)S(1)}, u32[]{:S(2)}, u32[]{:S(2)}) collective-permute-start(f32[32,32]{1,0:T(8,128)S(1)} %add.23), channel_id=1, source_target_pairs={{0,8},{1,9},{2,10},{3,11},{4,12},{5,13},{6,14},{7,15},{8,0},{9,1},... | collective-permute-start | bytes 12296 | tf_op jit(solution)/shard_map/ppermute | solution.py:178
  32.1 3.7 %collective-permute-start.1 = (bf16[32,2,4,128]{3,2,0,1:T(4,128)(2,1)S(1)}, bf16[32,2,4,128]{3,2,0,1:T(4,128)(2,1)S(1)}, u32[]{:S(2)}, u32[]{:S(2)}) collective-permute-start(bf16[32,2,4,128]{3,2,0,1:T(4,128)(2,1)S(1)} %broadcast_select_fusion), channel_id=1, source_target_pairs={{0,1},{1,0},{2,3},{3,2},{4,5},{5,4},{6,7},{7,6},{8,9},{9,8},{10,11... | collective-permute-start | bytes 196616 | tf_op jit(solution)/shard_map/ppermute | solution.py:178

commit v3 on v2

v3 whole, which is shorter than its diff:
```python
import functools

import jax
import jax.numpy as jnp
from jax import lax
from jax.experimental import pallas as pl
from jax.experimental.pallas import tpu as pltpu
from jax.sharding import PartitionSpec as P

REGIONS = 8
STEPS = 4
TILE = 8
SHARED = 2
CHUNK = 4
UNROLL = 7

lam_space = 0.2
lam_time = 0.08

LIMIT = 48 * 1024 * 1024


def phi(difference):
    return difference / (1.0 + difference * difference)


class Plan:
    def __init__(self, devices, date_dev, bands, rows):
        self.devices, self.date_dev, self.bands, self.rows = devices, date_dev, bands, rows
        self.dates = devices * date_dev
        planes = devices // bands
        self.shared = min(SHARED, planes)
        self.slabs = planes // self.shared
        self.plane_rows = rows // planes
        self.own_rows = rows // devices
        self.slab_rows = rows // self.slabs
        self.window = self.slab_rows + TILE * min(self.slabs - 1, 2)
        self.compact = self.slabs == 2 and date_dev == 2
        self.wire = 2 * self.slab_rows + TILE if self.compact else date_dev * self.window
        self.gram_blocks = max(1, 2 * self.dates // 128)
        self.gram_slots = self.gram_blocks * self.dates // self.own_rows

    def slab(self, index):
        return index // (self.bands * self.shared)

    def start(self, index):
        first = self.slab(index) * self.slab_rows - TILE
        last = self.rows - self.window
        if isinstance(index, int):
            return min(max(first, 0), last)
        return jnp.clip(first, 0, last)


def anomaly_kernel(plan, scenes_hbm, mask_hbm, region_hbm, send_ref, scenes_ref, mask_ref, region_ref, sums_ref, sems):
    date_dev, bands, rows, cols = scenes_ref.shape
    copies = [
        pltpu.make_async_copy(source, target, sems.at[i])
        for i, (source, target) in enumerate(
            ((scenes_hbm, scenes_ref), (mask_hbm, mask_ref), (region_hbm, region_ref))
        )
    ]
    for copy in copies:
        copy.start()
    for copy in copies:
        copy.wait()

    step = 2 * TILE
    tiles = rows // step
    per_region = bands + 1

    def tile_rows(i):
        return pl.ds(pl.multiple_of(i * step, step), step)

    for date in range(date_dev):

        def fold(x):
            return x[:TILE] + x[TILE:]

        def gather(i, sums):
            clear = mask_ref[date, tile_rows(i)] > 0
            label = jnp.where(clear, region_ref[tile_rows(i)], -1)
            values = [scenes_ref[date, band, tile_rows(i)].astype(jnp.float32) for band in range(bands)]
            out = []
            for g in range(REGIONS):
                here = label == g
                for band in range(bands):
                    out.append(sums[g * per_region + band] + fold(jnp.where(here, values[band], 0.0)))
                out.append(sums[g * per_region + bands] + fold(jnp.where(here, 1.0, 0.0)))
            return tuple(out)

        zero = jnp.zeros((TILE, cols), jnp.float32)
        sums = lax.fori_loop(0, tiles, gather, (zero,) * (REGIONS * per_region), unroll=min(tiles, 4))
        for i, total in enumerate(sums):
            sums_ref[date, i : i + 1] = jnp.sum(total, axis=0, keepdims=True)

    means = []
    for date in range(date_dev):
        totals = jnp.sum(sums_ref[date], axis=1, keepdims=True)
        for band in range(bands):
            means.append(
                [
                    totals[g * per_region + band : g * per_region + band + 1]
                    / (totals[g * per_region + bands : g * per_region + bands + 1] + 1.0)
                    for g in range(REGIONS)
                ]
            )

    region = region_ref[...]
    row = lax.broadcasted_iota(jnp.int32, (TILE, cols), 0)
    half = TILE // 2
    for band in range(bands):
        anomalies = []
        for date in range(date_dev):
            mean = jnp.zeros((rows, cols), jnp.float32)
            for g in range(REGIONS):
                mean = jnp.where(region == g, jnp.broadcast_to(means[date * bands + band][g], (rows, cols)), mean)
            clear = mask_ref[date].astype(jnp.float32)
            anomalies.append(clear * (scenes_ref[date, band].astype(jnp.float32) - mean))
        for target in range(band, plan.devices, bands):
            if plan.compact:
                slab, size = plan.slab(target), plan.slab_rows
                for date in range(date_dev):
                    send_ref[target, date * size : (date + 1) * size] = anomalies[date][
                        slab * size : (slab + 1) * size
                    ].astype(jnp.bfloat16)
                edge = size if slab == 0 else size - TILE
                wanted = row < half if slab == 0 else row >= half
                send_ref[target, 2 * size :] = jnp.where(
                    wanted,
                    anomalies[0][edge : edge + TILE],
                    pltpu.roll(anomalies[1][edge : edge + TILE], half, 0),
                ).astype(jnp.bfloat16)
            else:
                first, size = plan.start(target), plan.window
                for date in range(date_dev):
                    send_ref[target, date * size : (date + 1) * size] = anomalies[date][first : first + size].astype(
                        jnp.bfloat16
                    )


def store_gram(plan, slots_ref, first, gram):
    dates, own = plan.dates, plan.own_rows
    high = gram.astype(jnp.bfloat16).astype(jnp.float32)
    both = jnp.concatenate([high, gram - high], axis=1)
    width = min(2 * dates, 128)
    for block in range(plan.gram_blocks):
        part = both[:, block * width : (block + 1) * width].astype(jnp.bfloat16)
        for i in range(dates // own):
            slots_ref[first + block * (dates // own) + i, :, :width] = part[i * own : (i + 1) * own]


def load_gram(plan, slots_ref, first):
    dates, own = plan.dates, plan.own_rows
    width = min(2 * dates, 128)
    blocks = []
    for block in range(plan.gram_blocks):
        slots = [
            slots_ref[first + block * (dates // own) + i, :, :width].astype(jnp.float32)
            for i in range(dates // own)
        ]
        blocks.append(jnp.concatenate(slots, axis=0))
    both = blocks[0] if len(blocks) == 1 else jnp.concatenate(blocks, axis=1)
    return both[:, :dates] + both[:, dates:]


def diffuse_kernel(plan, got_ref, region_ref, message_ref, rest_ref, gram_ref, field_ref):
    window, dates, cols = plan.window, plan.dates, got_ref.shape[-1]
    me = lax.axis_index("dates")
    start = plan.start(me)
    slab_first = plan.slab(me) * plan.slab_rows - start
    land = (region_ref[pl.ds(pl.multiple_of(start, TILE), window)] > 0).astype(jnp.float32)
    row = lax.broadcasted_iota(jnp.int32, (window, cols), 0)
    col = lax.broadcasted_iota(jnp.int32, (window, cols), 1)
    down = jnp.where(row < window - 1, pltpu.roll(land, window - 1, 0), 0.0)
    right = jnp.where(col < cols - 1, pltpu.roll(land, cols - 1, 1), 0.0)
    row_weight = jnp.concatenate([lam_space * land * down] * CHUNK, axis=0)
    col_weight = jnp.concatenate([lam_space * land * right] * CHUNK, axis=0)
    source = lax.broadcasted_iota(jnp.int32, (cols, cols), 0)
    target = lax.broadcasted_iota(jnp.int32, (cols, cols), 1)
    same = (source == target).astype(jnp.float32)
    onward = ((source == target + 1).astype(jnp.float32) - same).astype(jnp.bfloat16)
    inflow = (same - (source + 1 == target).astype(jnp.float32)).astype(jnp.bfloat16)
    length, chunks = CHUNK * window, dates // CHUNK

    if plan.compact:
        size, half = plan.slab_rows, TILE // 2
        edge = jnp.where(slab_first == 0, size, 0)
        tile_row = lax.broadcasted_iota(jnp.int32, (TILE, cols), 0)
        wanted = (tile_row < half) == (slab_first == 0)
        for device in range(plan.devices):
            halos = got_ref[device, 2 * size :].astype(jnp.float32)
            for date, halo in enumerate((halos, pltpu.roll(halos, half, 0))):
                base = (2 * device + date) * window
                field_ref[pl.ds(pl.multiple_of(base + slab_first, TILE), size)] = got_ref[
                    device, date * size : (date + 1) * size
                ].astype(jnp.float32)
                field_ref[pl.ds(pl.multiple_of(base + edge, TILE), TILE)] = jnp.where(wanted, halo, 0.0)
    else:

        def unpack(device, carry):
            field_ref[pl.ds(pl.multiple_of(device * plan.wire, TILE), plan.wire)] = got_ref[device].astype(jnp.float32)
            return carry

        lax.fori_loop(0, plan.devices, unpack, 0)

    for step in range(STEPS):

        def read(t):
            return field_ref[pl.ds(pl.multiple_of(t * window, TILE), length)]

        def advance(current, following, date_in):
            difference = jnp.dot(current.astype(jnp.bfloat16), onward, preferred_element_type=jnp.float32)
            col_flux = (col_weight * phi(difference)).astype(jnp.bfloat16)
            row_flux = row_weight * phi(pltpu.roll(current, length - 1, 0) - current)
            date_flux = lam_time * phi(following - current)
            new = (
                current
                + (row_flux - pltpu.roll(row_flux, 1, 0))
                + jnp.dot(col_flux, inflow, preferred_element_type=jnp.float32)
                + (date_flux - jnp.concatenate([date_in, date_flux[:-window]], axis=0))
            )
            return new, date_flux[-window:]

        def one(k, date_in):
            new, date_out = advance(read(k * CHUNK), read(k * CHUNK + 1), date_in)
            field_ref[pl.ds(pl.multiple_of(k * length, TILE), length)] = new
            return date_out

        date_in = lax.fori_loop(
            0, chunks - 1, one, jnp.zeros((window, cols), jnp.float32), unroll=min(chunks - 1, UNROLL)
        )
        current = read((chunks - 1) * CHUNK)
        new, _ = advance(current, jnp.concatenate([current[window:], current[-window:]], axis=0), date_in)
        field_ref[pl.ds((chunks - 1) * length, length)] = new

    def gram_rows(i, total):
        rows = jnp.concatenate(
            [field_ref[pl.ds(slab_first + 2 * i + j, dates, stride=window)] for j in range(2)], axis=1
        ).astype(jnp.bfloat16)
        return total + lax.dot_general(
            rows, rows, (((1,), (1,)), ((), ())), preferred_element_type=jnp.float32
        )

    gram = lax.fori_loop(
        0, plan.slab_rows // 2, gram_rows, jnp.zeros((dates, dates), jnp.float32), unroll=min(8, plan.slab_rows // 2)
    )
    gram_ref[...] = gram
    store_gram(plan, message_ref, 2 * dates, gram)

    own = plan.own_rows
    place = me % plan.bands
    plane_first = (me // plan.bands) * plan.plane_rows - start

    def share(t, carry):
        for ref, slot, other in (
            (message_ref, t, 3), (message_ref, dates + t, 2), (rest_ref, t, 0), (rest_ref, dates + t, 1)
        ):
            first = plane_first + (place ^ other) * own
            ref[slot] = field_ref[pl.ds(t * window + first, own)].astype(jnp.bfloat16)
        return carry

    lax.fori_loop(0, dates, share, 0, unroll=8)


def relay_kernel(plan, got_ref, rest_ref, gram_ref, message_ref, total_ref):
    dates = plan.dates
    message_ref[:dates] = rest_ref[dates:]
    message_ref[dates : 2 * dates] = got_ref[dates : 2 * dates]
    total = gram_ref[...] + load_gram(plan, got_ref, 2 * dates)
    total_ref[...] = total
    store_gram(plan, message_ref, 2 * dates, total)


def total_kernel(plan, got_ref, gram_ref, total_ref):
    total_ref[...] = gram_ref[...] + load_gram(plan, got_ref, 2 * plan.dates)


def assemble_kernel(plan, rest_ref, first_ref, second_ref, out_ref):
    dates = plan.dates
    place = lax.axis_index("dates") % plan.bands
    out_ref[:, place] = rest_ref[:dates]
    out_ref[:, place ^ 3] = first_ref[:dates]
    out_ref[:, place ^ 1] = second_ref[:dates]
    out_ref[:, place ^ 2] = second_ref[dates : 2 * dates]


def swap(x, bits):
    count = lax.axis_size("dates")
    return lax.ppermute(x, "dates", [(i, i ^ bits) for i in range(count)])


def local(scenes, cloud_mask, region):
    date_dev, bands, rows, cols = scenes.shape
    devices = lax.axis_size("dates")
    plan = Plan(devices, date_dev, bands, rows)
    dates, own = plan.dates, plan.own_rows
    me = lax.axis_index("dates")
    vmem = pl.BlockSpec(memory_space=pltpu.VMEM)
    hbm = pl.BlockSpec(memory_space=pltpu.MemorySpace.HBM)
    params = pltpu.CompilerParams(vmem_limit_bytes=LIMIT)

    def shape(*sizes, dtype=jnp.bfloat16):
        return jax.ShapeDtypeStruct(sizes, dtype)

    send = pl.pallas_call(
        functools.partial(anomaly_kernel, plan),
        out_shape=shape(devices, plan.wire, cols),
        in_specs=[hbm] * 3,
        out_specs=vmem,
        scratch_shapes=[
            pltpu.VMEM(scenes.shape, scenes.dtype),
            pltpu.VMEM(cloud_mask.shape, cloud_mask.dtype),
            pltpu.VMEM(region.shape, region.dtype),
            pltpu.VMEM((date_dev, REGIONS * (bands + 1), cols), jnp.float32),
            pltpu.SemaphoreType.DMA((3,)),
        ],
        compiler_params=params,
    )(*(pltpu.with_memory_space_constraint(x, pltpu.MemorySpace.HBM) for x in (scenes, cloud_mask, region)))
    got = lax.all_to_all(send, "dates", split_axis=0, concat_axis=0, tiled=True)
    slots = 2 * dates + plan.gram_slots
    square = shape(dates, dates, dtype=jnp.float32)
    message, rest, gram = pl.pallas_call(
        functools.partial(diffuse_kernel, plan),
        out_shape=(shape(slots, own, cols), shape(2 * dates, own, cols), square),
        in_specs=[vmem] * 2,
        out_specs=(vmem,) * 3,
        scratch_shapes=[pltpu.VMEM((dates * plan.window, cols), jnp.float32)],
        compiler_params=params,
    )(got, region)
    first = swap(message, 3)
    message, gram = pl.pallas_call(
        functools.partial(relay_kernel, plan),
        out_shape=(shape(slots, own, cols), square),
        in_specs=[vmem] * 3,
        out_specs=(vmem,) * 2,
        compiler_params=params,
    )(first, rest, gram)
    second = swap(message, 1)
    gram = pl.pallas_call(
        functools.partial(total_kernel, plan),
        out_shape=square,
        in_specs=[vmem] * 2,
        out_specs=vmem,
        compiler_params=params,
    )(second, gram)

    bit = bands * plan.shared
    while 2 * bit < devices:
        gram = gram + swap(gram, bit + 1)
        bit *= 2

    def rows_of(index):
        return lax.dynamic_slice_in_dim(gram, index * date_dev, date_dev, 0)

    mine = rows_of(me)
    if bit < devices:
        mine = mine + swap(rows_of(me ^ (bit + 1)), bit + 1)
    smoothed = pl.pallas_call(
        functools.partial(assemble_kernel, plan),
        out_shape=shape(dates, bands, own, cols),
        in_specs=[vmem] * 3,
        out_specs=vmem,
        compiler_params=params,
        cost_estimate=pl.CostEstimate(flops=dates * bands * own * cols, bytes_accessed=dates * bands * own * cols * 4, transcendentals=0),
    )(rest, first, second)
    return smoothed, mine / (bands * rows * cols)


def solution(mesh):
    in_specs = (
        P(("groups", "dates"), None, None, None),
        P(("groups", "dates"), None, None),
        P("groups", None),
    )
    out_specs = (P("groups", None, "dates", None), P(("groups", "dates"), None))
    return jax.shard_map(local, mesh=mesh, in_specs=in_specs, out_specs=out_specs, check_vma=False)
```

time: 37.1 us -> 33.8 us (0.911)
  local copies, waits for them, and re-layouts: 3.24 us -> 0.01 us
  starting transfers between devices: 3.53 us -> 1.26 us
  Pallas kernels: 3.47 us -> 5.54 us
  waiting for transfers between devices: 6.67 us -> 7.82 us
  blocking collectives: 18.3 us -> 17.8 us
    unnamed x9 -> x2, local copies, waits for them, and re-layouts: 3.22 us -> 0.01 us
    ppermute x5 -> x3, starting transfers between devices: 3.53 us -> 1.26 us  [swap(): return lax.ppermute(x, 'dates', [(i, i ^ bits) for i in range(count)])]
    pallas_call x2 -> x5, Pallas kernels: 3.47 us -> 5.54 us  [the longest x1 3.12 us: local(): pl.pallas_call(functools.partial(diffuse_kernel, plan), out_shape=(shape(...]
    ppermute x5 -> x3, waiting for transfers between devices: 6.67 us -> 7.82 us  [swap(): return lax.ppermute(x, 'dates', [(i, i ^ bits) for i in range(count)])]
    all_to_all x1, blocking collectives: 18.3 us -> 17.8 us  [local(): got = lax.all_to_all(send, 'dates', split_axis=0, concat_axis=0, tiled=True)]
  transfers between devices with their start and end apart: 5 -> 3, of which waited for: 3 -> 3; matrix products, arithmetic and copies ran while one was open for 2% -> 0% of each run, Pallas kernels for 0% -> 2%
where the time goes in v3:
time: 33.8 us; the launch traced here: 33.6 us
  blocking collectives  17.8 us (53%)
  waiting for transfers between devices  7.82 us (23%)
  Pallas kernels  5.54 us (16%)
  starting transfers between devices  1.26 us (4%)
  between operations  0.66 us (2%)
  other arithmetic  0.57 us (2%)
    all_to_all x1, blocking collectives, local(): got = lax.all_to_all(send, 'dates', split_axis=0, concat_axis=0, tiled=True)  17.8 us
    ppermute x3, waiting for transfers between devices, swap(): return lax.ppermute(x, 'dates', [(i, i ^ bits) for i in range(count)])  7.82 us
    pallas_call x1, Pallas kernels, local(): pl.pallas_call(functools.partial(diffuse_kernel, plan), out_shape=(shape(...  3.12 us
    pallas_call x1, Pallas kernels, local(): pl.pallas_call(functools.partial(anomaly_kernel, plan), out_shape=shape(d...  1.49 us
    ppermute x3, starting transfers between devices, swap(): return lax.ppermute(x, 'dates', [(i, i ^ bits) for i in range(count)])  1.26 us
    pallas_call x1, Pallas kernels, local(): pl.pallas_call(functools.partial(assemble_kernel, plan), out_shape=shape(...  0.7 us
  transfers between devices with their start and end apart: 3, of which 3 were waited for; matrix products, arithmetic and copies ran while one was open for 0% of the time, Pallas kernels for 2%

profile of v3, /device:TPU:0, one launch (start us, length us, event | category | flops | bytes accessed | tf_op | source)
XLA Modules:
  0.0 33.6 jit_solution(16696444380060338796)
XLA Ops:
  0.6 1.5 %shard_map.50 = bf16[16,72,128]{2,1,0:T(8,128)(2,1)S(1)} custom-call(bf16[2,4,64,128]{3,2,1,0:T(8,128)(2,1)} %scenes_hbm.1, s32[2,64,128]{2,1,0:T(8,128)} %mask_hbm.1, s32[64,128]{1,0:T(8,128)} %region_ref.1), custom_call_target="tpu_custom_call" | custom-call | tf_op jit(solution)/shard_map/pallas_call | solution.py:305
  2.1 0.0 copy-start
  2.1 17.8 %all_to_all.5.got_ref = bf16[16,72,128]{2,1,0:T(8,128)(2,1)S(1)} all-to-all(bf16[16,72,128]{2,1,0:T(8,128)(2,1)S(1)} %shard_map.50), channel_id=1, replica_groups=mesh['groups'=2,'dates'=16] {'dates'}, dimensions={0} | all-to-all | bytes 589824 | tf_op jit(solution)/shard_map/all_to_all | solution.py:319
  19.9 0.0 copy-done
  19.9 3.1 %shard_map.51 = (bf16[72,4,128]{2,1,0:T(4,128)(2,1)S(1)}, bf16[64,4,128]{2,1,0:T(4,128)(2,1)S(1)}, f32[32,32]{1,0:T(8,128)S(1)}) custom-call(bf16[16,72,128]{2,1,0:T(8,128)(2,1)S(1)} %all_to_all.5.got_ref, s32[64,128]{1,0:T(8,128)S(1)} %copy-done), custom_call_target="tpu_custom_call" | custom-call | tf_op jit(solution)/shard_map/pallas_call | solution.py:322
  23.0 0.3 collective-permute-start
  23.4 4.2 %collective-permute-done.got_ref.first_ref = bf16[72,4,128]{2,1,0:T(4,128)(2,1)S(1)} collective-permute-done((bf16[72,4,128]{2,1,0:T(4,128)(2,1)S(1)}, bf16[72,4,128]{2,1,0:T(4,128)(2,1)S(1)}, u32[]{:S(2)}, u32[]{:S(2)}) %collective-permute-start) | collective-permute-done | bytes 73760 | tf_op jit(solution)/shard_map/ppermute | solution.py:289
  27.6 0.2 shard_map.52
  27.8 0.1 collective-permute-start.1
  27.9 1.2 %collective-permute-done.1.second_ref.got_ref = bf16[72,4,128]{2,1,0:T(4,128)(2,1)S(1)} collective-permute-done((bf16[72,4,128]{2,1,0:T(4,128)(2,1)S(1)}, bf16[72,4,128]{2,1,0:T(4,128)(2,1)S(1)}, u32[]{:S(2)}, u32[]{:S(2)}) %collective-permute-start.1) | collective-permute-done | bytes 73760 | tf_op jit(solution)/shard_map/ppermute | solution.py:289
  29.0 0.1 shard_map.54
  29.1 0.8 %collective-permute-start.2 = (f32[2,32]{1,0:T(2,128)S(1)}, f32[2,32]{1,0:T(2,128)S(1)}, u32[]{:S(2)}, u32[]{:S(2)}) collective-permute-start(f32[2,32]{1,0:T(2,128)S(1)} %constant_dynamic-slice_fusion), channel_id=1, source_target_pairs={{0,9},{1,8},{2,11},{3,10},{4,13},{5,12},{6,15},{7,14},{8,1},{9,0},... | collective-permute-start | bytes 776 | tf_op jit(solution)/shard_map/ppermute | solution.py:289
  29.9 0.7 %shard_map.53 = bf16[32,4,4,128]{3,2,1,0:T(4,128)(2,1)} custom-call(bf16[64,4,128]{2,1,0:T(4,128)(2,1)S(1)} %get-tuple-element.7.rest_ref, bf16[72,4,128]{2,1,0:T(4,128)(2,1)S(1)} %collective-permute-done.got_ref.first_ref, bf16[72,4,128]{2,1,0:T(4,128)(2,1)S(1)} %collective-permute-done.1.second_ref.got_ref), custom_call_target="tpu_custom_call" | custom-call | flops 65536 | bytes 262144 | tf_op jit(solution)/shard_map/pallas_call | solution.py:358
  30.6 2.4 %collective-permute-done.2 = f32[2,32]{1,0:T(2,128)S(1)} collective-permute-done((f32[2,32]{1,0:T(2,128)S(1)}, f32[2,32]{1,0:T(2,128)S(1)}, u32[]{:S(2)}, u32[]{:S(2)}) %collective-permute-start.2) | collective-permute-done | bytes 288 | tf_op jit(solution)/shard_map/ppermute | solution.py:289
  33.0 0.6 %add_multiply_fusion = f32[2,32]{1,0:T(2,128)} fusion(f32[2,32]{1,0:T(2,128)S(1)} %collective-permute-done.2, f32[32,32]{1,0:T(8,128)S(1)} %shard_map.54, s32[]{:T(128)S(6)} %select_n.6), kind=kLoop, calls=%fused_computation | loop fusion | flops 128 | bytes 772 | tf_op jit(solution)/shard_map/div | solution.py:366
  (1 shorter events, 0.0 us)
Async XLA Ops:
  2.1 17.8 %copy-start = (s32[64,128]{1,0:T(8,128)S(1)}, s32[64,128]{1,0:T(8,128)}, u32[]{:S(2)}) copy-start(s32[64,128]{1,0:T(8,128)} %region_ref.1) | copy-start | bytes 98308
  23.0 4.6 %collective-permute-start = (bf16[72,4,128]{2,1,0:T(4,128)(2,1)S(1)}, bf16[72,4,128]{2,1,0:T(4,128)(2,1)S(1)}, u32[]{:S(2)}, u32[]{:S(2)}) collective-permute-start(bf16[72,4,128]{2,1,0:T(4,128)(2,1)S(1)} %get-tuple-element.8), channel_id=1, source_target_pairs={{0,3},{1,2},{2,1},{3,0},{4,7},{5,6},{6,5},{7,4},{8,11},{9,10},{10,... | collective-permute-start | bytes 221192 | tf_op jit(solution)/shard_map/ppermute | solution.py:289
  27.8 1.3 %collective-permute-start.1 = (bf16[72,4,128]{2,1,0:T(4,128)(2,1)S(1)}, bf16[72,4,128]{2,1,0:T(4,128)(2,1)S(1)}, u32[]{:S(2)}, u32[]{:S(2)}) collective-permute-start(bf16[72,4,128]{2,1,0:T(4,128)(2,1)S(1)} %get-tuple-element.10), channel_id=1, source_target_pairs={{0,1},{1,0},{2,3},{3,2},{4,5},{5,4},{6,7},{7,6},{8,9},{9,8},{10,11... | collective-permute-start | bytes 221192 | tf_op jit(solution)/shard_map/ppermute | solution.py:289
  29.1 3.9 %collective-permute-start.2 = (f32[2,32]{1,0:T(2,128)S(1)}, f32[2,32]{1,0:T(2,128)S(1)}, u32[]{:S(2)}, u32[]{:S(2)}) collective-permute-start(f32[2,32]{1,0:T(2,128)S(1)} %constant_dynamic-slice_fusion), channel_id=1, source_target_pairs={{0,9},{1,8},{2,11},{3,10},{4,13},{5,12},{6,15},{7,14},{8,1},{9,0},... | collective-permute-start | bytes 776 | tf_op jit(solution)/shard_map/ppermute | solution.py:289

commit v4 on v3

--- a/solution.py
+++ b/solution.py
@@ -18,6 +18,7 @@
 lam_time = 0.08
 
 LIMIT = 48 * 1024 * 1024
+HEAVY = 10**10
 
 
 def phi(difference):
@@ -37,8 +38,6 @@
         self.window = self.slab_rows + TILE * min(self.slabs - 1, 2)
         self.compact = self.slabs == 2 and date_dev == 2
         self.wire = 2 * self.slab_rows + TILE if self.compact else date_dev * self.window
-        self.gram_blocks = max(1, 2 * self.dates // 128)
-        self.gram_slots = self.gram_blocks * self.dates // self.own_rows
 
     def slab(self, index):
         return index // (self.bands * self.shared)
@@ -138,32 +137,7 @@
                     )
 
 
-def store_gram(plan, slots_ref, first, gram):
-    dates, own = plan.dates, plan.own_rows
-    high = gram.astype(jnp.bfloat16).astype(jnp.float32)
-    both = jnp.concatenate([high, gram - high], axis=1)
-    width = min(2 * dates, 128)
-    for block in range(plan.gram_blocks):
-        part = both[:, block * width : (block + 1) * width].astype(jnp.bfloat16)
-        for i in range(dates // own):
-            slots_ref[first + block * (dates // own) + i, :, :width] = part[i * own : (i + 1) * own]
-
-
-def load_gram(plan, slots_ref, first):
-    dates, own = plan.dates, plan.own_rows
-    width = min(2 * dates, 128)
-    blocks = []
-    for block in range(plan.gram_blocks):
-        slots = [
-            slots_ref[first + block * (dates // own) + i, :, :width].astype(jnp.float32)
-            for i in range(dates // own)
-        ]
-        blocks.append(jnp.concatenate(slots, axis=0))
-    both = blocks[0] if len(blocks) == 1 else jnp.concatenate(blocks, axis=1)
-    return both[:, :dates] + both[:, dates:]
-
-
-def diffuse_kernel(plan, got_ref, region_ref, message_ref, rest_ref, gram_ref, field_ref):
+def diffuse_kernel(plan, got_ref, region_ref, gram_ref, field_ref):
     window, dates, cols = plan.window, plan.dates, got_ref.shape[-1]
     me = lax.axis_index("dates")
     start = plan.start(me)
@@ -241,15 +215,16 @@
             rows, rows, (((1,), (1,)), ((), ())), preferred_element_type=jnp.float32
         )
 
-    gram = lax.fori_loop(
+    gram_ref[...] = lax.fori_loop(
         0, plan.slab_rows // 2, gram_rows, jnp.zeros((dates, dates), jnp.float32), unroll=min(8, plan.slab_rows // 2)
     )
-    gram_ref[...] = gram
-    store_gram(plan, message_ref, 2 * dates, gram)
-
-    own = plan.own_rows
+
+
+def share_kernel(plan, field_ref, gram_ref, message_ref, rest_ref):
+    window, dates, own = plan.window, plan.dates, plan.own_rows
+    me = lax.axis_index("dates")
     place = me % plan.bands
-    plane_first = (me // plan.bands) * plan.plane_rows - start
+    plane_first = (me // plan.bands) * plan.plane_rows - plan.start(me)
 
     def share(t, carry):
         for ref, slot, other in (
@@ -262,26 +237,32 @@
     lax.fori_loop(0, dates, share, 0, unroll=8)
 
 
-def relay_kernel(plan, got_ref, rest_ref, gram_ref, message_ref, total_ref):
+def relay_kernel(plan, got_ref, rest_ref, message_ref):
     dates = plan.dates
     message_ref[:dates] = rest_ref[dates:]
-    message_ref[dates : 2 * dates] = got_ref[dates : 2 * dates]
-    total = gram_ref[...] + load_gram(plan, got_ref, 2 * dates)
-    total_ref[...] = total
-    store_gram(plan, message_ref, 2 * dates, total)
-
-
-def total_kernel(plan, got_ref, gram_ref, total_ref):
-    total_ref[...] = gram_ref[...] + load_gram(plan, got_ref, 2 * plan.dates)
-
-
-def assemble_kernel(plan, rest_ref, first_ref, second_ref, out_ref):
+    message_ref[dates:] = got_ref[dates:]
+
+
+def sum_kernel(scale, mine_ref, other_ref, sim_ref):
+    sim_ref[...] = (mine_ref[...] + other_ref[...]) * scale
+
+
+def finish_kernel(plan, rest_ref, first_ref, second_ref, sim_ref, out_hbm, sim_hbm, sems):
     dates = plan.dates
     place = lax.axis_index("dates") % plan.bands
-    out_ref[:, place] = rest_ref[:dates]
-    out_ref[:, place ^ 3] = first_ref[:dates]
-    out_ref[:, place ^ 1] = second_ref[:dates]
-    out_ref[:, place ^ 2] = second_ref[dates : 2 * dates]
+    head, tail = pl.ds(0, dates), pl.ds(dates, dates)
+    copies = [
+        pltpu.make_async_copy(source.at[part], out_hbm.at[:, place ^ other], sems.at[i])
+        for i, (source, part, other) in enumerate(
+            ((rest_ref, head, 0), (first_ref, head, 3), (second_ref, head, 1), (second_ref, tail, 2))
+        )
+    ]
+    for copy in copies:
+        copy.start()
+    copies.append(pltpu.make_async_copy(sim_ref, sim_hbm, sems.at[4]))
+    copies[-1].start()
+    for copy in copies:
+        copy.wait()
 
 
 def swap(x, bits):
@@ -298,6 +279,8 @@
     vmem = pl.BlockSpec(memory_space=pltpu.VMEM)
     hbm = pl.BlockSpec(memory_space=pltpu.MemorySpace.HBM)
     params = pltpu.CompilerParams(vmem_limit_bytes=LIMIT)
+    moved = dates * bands * own * cols
+    small = pl.CostEstimate(flops=moved, bytes_accessed=4 * moved, transcendentals=0)
 
     def shape(*sizes, dtype=jnp.bfloat16):
         return jax.ShapeDtypeStruct(sizes, dtype)
@@ -317,32 +300,25 @@
         compiler_params=params,
     )(*(pltpu.with_memory_space_constraint(x, pltpu.MemorySpace.HBM) for x in (scenes, cloud_mask, region)))
     got = lax.all_to_all(send, "dates", split_axis=0, concat_axis=0, tiled=True)
-    slots = 2 * dates + plan.gram_slots
-    square = shape(dates, dates, dtype=jnp.float32)
-    message, rest, gram = pl.pallas_call(
+    gram, field = pl.pallas_call(
         functools.partial(diffuse_kernel, plan),
-        out_shape=(shape(slots, own, cols), shape(2 * dates, own, cols), square),
+        out_shape=(shape(dates, dates, dtype=jnp.float32), shape(dates * plan.window, cols, dtype=jnp.float32)),
         in_specs=[vmem] * 2,
-        out_specs=(vmem,) * 3,
-        scratch_shapes=[pltpu.VMEM((dates * plan.window, cols), jnp.float32)],
+        out_specs=(vmem,) * 2,
         compiler_params=params,
     )(got, region)
+    gram = gram + swap(gram, 3)
+    rows_shape = shape(2 * dates, own, cols)
+    message, rest = pl.pallas_call(
+        functools.partial(share_kernel, plan),
+        out_shape=(rows_shape, rows_shape),
+        in_specs=[vmem] * 2,
+        out_specs=(vmem,) * 2,
+        compiler_params=params,
+        cost_estimate=small,
+    )(field, gram)
     first = swap(message, 3)
-    message, gram = pl.pallas_call(
-        functools.partial(relay_kernel, plan),
-        out_shape=(shape(slots, own, cols), square),
-        in_specs=[vmem] * 3,
-        out_specs=(vmem,) * 2,
-        compiler_params=params,
-    )(first, rest, gram)
-    second = swap(message, 1)
-    gram = pl.pallas_call(
-        functools.partial(total_kernel, plan),
-        out_shape=square,
-        in_specs=[vmem] * 2,
-        out_specs=vmem,
-        compiler_params=params,
-    )(second, gram)
+    gram = gram + swap(gram, 1)
 
     bit = bands * plan.shared
     while 2 * bit < devices:
@@ -353,17 +329,33 @@
         return lax.dynamic_slice_in_dim(gram, index * date_dev, date_dev, 0)
 
     mine = rows_of(me)
-    if bit < devices:
-        mine = mine + swap(rows_of(me ^ (bit + 1)), bit + 1)
-    smoothed = pl.pallas_call(
-        functools.partial(assemble_kernel, plan),
-        out_shape=shape(dates, bands, own, cols),
-        in_specs=[vmem] * 3,
+    other = swap(rows_of(me ^ (bit + 1)), bit + 1) if bit < devices else jnp.zeros_like(mine)
+    message = pl.pallas_call(
+        functools.partial(relay_kernel, plan),
+        out_shape=rows_shape,
+        in_specs=[vmem] * 2,
         out_specs=vmem,
         compiler_params=params,
-        cost_estimate=pl.CostEstimate(flops=dates * bands * own * cols, bytes_accessed=dates * bands * own * cols * 4, transcendentals=0),
-    )(rest, first, second)
-    return smoothed, mine / (bands * rows * cols)
+        cost_estimate=small,
+    )(first, rest)
+    second = swap(message, 1)
+    similarity = pl.pallas_call(
+        functools.partial(sum_kernel, 1.0 / (bands * rows * cols)),
+        out_shape=shape(date_dev, dates, dtype=jnp.float32),
+        in_specs=[vmem] * 2,
+        out_specs=vmem,
+        compiler_params=params,
+        cost_estimate=pl.CostEstimate(flops=HEAVY, bytes_accessed=HEAVY // 100, transcendentals=0),
+    )(mine, other)
+    return pl.pallas_call(
+        functools.partial(finish_kernel, plan),
+        out_shape=(shape(dates, bands, own, cols), shape(date_dev, dates, dtype=jnp.float32)),
+        in_specs=[vmem] * 4,
+        out_specs=(hbm,) * 2,
+        scratch_shapes=[pltpu.SemaphoreType.DMA((5,))],
+        compiler_params=params,
+        cost_estimate=small,
+    )(rest, first, second, similarity)
 
 
 def solution(mesh):

time: 33.8 us -> 32.6 us (0.964)
  waiting for transfers between devices: 7.82 us -> 6.86 us
  starting transfers between devices: 1.26 us -> 1.83 us
  other arithmetic: 0.57 us -> 0.01 us
    ppermute x3 -> x5, waiting for transfers between devices: 7.82 us -> 6.86 us  [swap(): return lax.ppermute(x, 'dates', [(i, i ^ bits) for i in range(count)])]
    ppermute x3 -> x5, starting transfers between devices: 1.26 us -> 1.83 us  [swap(): return lax.ppermute(x, 'dates', [(i, i ^ bits) for i in range(count)])]
    div x1 -> x0, other arithmetic: 0.57 us -> none  [local(): return (smoothed, mine / (bands * rows * cols))]
    pallas_call x3 -> x4, Pallas kernels: 0.94 us -> 0.76 us  [the longest x1 0.69 us: local(): pl.pallas_call(functools.partial(finish_kernel, plan), out_shape=(shape(d...]
  transfers between devices with their start and end apart: 3 -> 5, of which waited for: 3 -> 5; matrix products, arithmetic and copies ran while one was open for 0% -> 0% of each run, Pallas kernels for 2% -> 0%
where the time goes in v4:
time: 32.6 us; the launch traced here: 32.4 us
  blocking collectives  17.8 us (55%)
  waiting for transfers between devices  6.86 us (21%)
  Pallas kernels  5.24 us (16%)
  starting transfers between devices  1.83 us (6%)
  between operations  0.67 us (2%)
    all_to_all x1, blocking collectives, local(): got = lax.all_to_all(send, 'dates', split_axis=0, concat_axis=0, tiled=True)  17.8 us
    ppermute x5, waiting for transfers between devices, swap(): return lax.ppermute(x, 'dates', [(i, i ^ bits) for i in range(count)])  6.86 us
    pallas_call x1, Pallas kernels, local(): pl.pallas_call(functools.partial(diffuse_kernel, plan), out_shape=(shape(...  2.99 us
    ppermute x5, starting transfers between devices, swap(): return lax.ppermute(x, 'dates', [(i, i ^ bits) for i in range(count)])  1.83 us
    pallas_call x1, Pallas kernels, local(): pl.pallas_call(functools.partial(anomaly_kernel, plan), out_shape=shape(d...  1.49 us
    pallas_call x1, Pallas kernels, local(): pl.pallas_call(functools.partial(finish_kernel, plan), out_shape=(shape(d...  0.69 us
  transfers between devices with their start and end apart: 5, of which 5 were waited for; matrix products, arithmetic and copies ran while one was open for 0% of the time, Pallas kernels for 0%

profile of v4, /device:TPU:0, one launch (start us, length us, event | category | flops | bytes accessed | tf_op | source)
XLA Modules:
  0.0 32.4 jit_solution(17317356594582805703)
XLA Ops:
  0.6 1.5 %shard_map.50 = bf16[16,72,128]{2,1,0:T(8,128)(2,1)S(1)} custom-call(bf16[2,4,64,128]{3,2,1,0:T(8,128)(2,1)} %scenes_hbm.1, s32[2,64,128]{2,1,0:T(8,128)} %mask_hbm.1, s32[64,128]{1,0:T(8,128)} %region_ref.1), custom_call_target="tpu_custom_call" | custom-call | tf_op jit(solution)/shard_map/pallas_call | solution.py:288
  2.1 0.0 copy-start
  2.1 17.8 %all_to_all.5.got_ref = bf16[16,72,128]{2,1,0:T(8,128)(2,1)S(1)} all-to-all(bf16[16,72,128]{2,1,0:T(8,128)(2,1)S(1)} %shard_map.50), channel_id=1, replica_groups=mesh['groups'=2,'dates'=16] {'dates'}, dimensions={0} | all-to-all | bytes 589824 | tf_op jit(solution)/shard_map/all_to_all | solution.py:302
  19.9 0.0 copy-done
  19.9 3.0 %shard_map.51 = (f32[32,32]{1,0:T(8,128)S(1)}, f32[1280,128]{1,0:T(8,128)S(1)}) custom-call(bf16[16,72,128]{2,1,0:T(8,128)(2,1)S(1)} %all_to_all.5.got_ref, s32[64,128]{1,0:T(8,128)S(1)} %copy-done), custom_call_target="tpu_custom_call" | custom-call | tf_op jit(solution)/shard_map/pallas_call | solution.py:303
  22.9 0.3 collective-permute-start
  23.2 3.0 %collective-permute-done = f32[32,32]{1,0:T(8,128)S(1)} collective-permute-done((f32[32,32]{1,0:T(8,128)S(1)}, f32[32,32]{1,0:T(8,128)S(1)}, u32[]{:S(2)}, u32[]{:S(2)}) %collective-permute-start) | collective-permute-done | bytes 4128 | tf_op jit(solution)/shard_map/ppermute | solution.py:270
  26.2 0.1 collective-permute-start.3
  26.3 0.1 shard_map.52
  26.4 0.1 collective-permute-start.1
  26.5 0.9 %collective-permute-done.3 = f32[32,32]{1,0:T(8,128)S(1)} collective-permute-done((f32[32,32]{1,0:T(8,128)S(1)}, f32[32,32]{1,0:T(8,128)S(1)}, u32[]{:S(2)}, u32[]{:S(2)}) %collective-permute-start.3) | collective-permute-done | bytes 4128 | tf_op jit(solution)/shard_map/ppermute | solution.py:270
  27.4 1.0 %collective-permute-start.4 = (f32[2,32]{1,0:T(2,128)S(1)}, f32[2,32]{1,0:T(2,128)S(1)}, u32[]{:S(2)}, u32[]{:S(2)}) collective-permute-start(f32[2,32]{1,0:T(2,128)S(1)} %get-tuple-element.10), channel_id=1, source_target_pairs={{0,9},{1,8},{2,11},{3,10},{4,13},{5,12},{6,15},{7,14},{8,1},{9,0},... | collective-permute-start | bytes 776 | tf_op jit(solution)/shard_map/ppermute | solution.py:270
  28.4 2.0 %collective-permute-done.1.got_ref.first_ref = bf16[64,4,128]{2,1,0:T(4,128)(2,1)S(1)} collective-permute-done((bf16[64,4,128]{2,1,0:T(4,128)(2,1)S(1)}, bf16[64,4,128]{2,1,0:T(4,128)(2,1)S(1)}, u32[]{:S(2)}, u32[]{:S(2)}) %collective-permute-start.1) | collective-permute-done | bytes 65568 | tf_op jit(solution)/shard_map/ppermute | solution.py:270
  30.4 0.3 collective-permute-start.2
  30.7 0.7 %collective-permute-done.4.other_ref = f32[2,32]{1,0:T(2,128)S(1)} collective-permute-done((f32[2,32]{1,0:T(2,128)S(1)}, f32[2,32]{1,0:T(2,128)S(1)}, u32[]{:S(2)}, u32[]{:S(2)}) %collective-permute-start.4) | collective-permute-done | bytes 288 | tf_op jit(solution)/shard_map/ppermute | solution.py:270
  31.4 0.3 collective-permute-done.2.second_ref
  31.7 0.7 %shard_map.55 = (bf16[32,4,4,128]{3,2,1,0:T(4,128)(2,1)}, f32[2,32]{1,0:T(2,128)}) custom-call(bf16[64,4,128]{2,1,0:T(4,128)(2,1)S(1)} %get-tuple-element.8.rest_ref, bf16[64,4,128]{2,1,0:T(4,128)(2,1)S(1)} %collective-permute-done.1.got_ref.first_ref, bf16[64,4,128]{2,1,0:T(4,128)(2,1)S(1)} %collective-permute-done.2.second_ref, f32[2,32]{1,0:T(2,128)S(1)} %shard_map.54.sim_ref), custom_call_target="tpu_custom_call" | custom-call | flops 65536 | bytes 262144 | tf_op jit(solution)/shard_map/pallas_call | solution.py:350
  (5 shorter events, 0.0 us)
Async XLA Ops:
  2.1 17.8 %copy-start = (s32[64,128]{1,0:T(8,128)S(1)}, s32[64,128]{1,0:T(8,128)}, u32[]{:S(2)}) copy-start(s32[64,128]{1,0:T(8,128)} %region_ref.1) | copy-start | bytes 98308
  22.9 3.3 %collective-permute-start = (f32[32,32]{1,0:T(8,128)S(1)}, f32[32,32]{1,0:T(8,128)S(1)}, u32[]{:S(2)}, u32[]{:S(2)}) collective-permute-start(f32[32,32]{1,0:T(8,128)S(1)} %get-tuple-element.7), channel_id=1, source_target_pairs={{0,3},{1,2},{2,1},{3,0},{4,7},{5,6},{6,5},{7,4},{8,11},{9,10},{10,... | collective-permute-start | bytes 12296 | tf_op jit(solution)/shard_map/ppermute | solution.py:270
  26.2 1.2 %collective-permute-start.3 = (f32[32,32]{1,0:T(8,128)S(1)}, f32[32,32]{1,0:T(8,128)S(1)}, u32[]{:S(2)}, u32[]{:S(2)}) collective-permute-start(f32[32,32]{1,0:T(8,128)S(1)} %add.12.gram_ref), channel_id=1, source_target_pairs={{0,1},{1,0},{2,3},{3,2},{4,5},{5,4},{6,7},{7,6},{8,9},{9,8},{10,11... | collective-permute-start | bytes 12296 | tf_op jit(solution)/shard_map/ppermute | solution.py:270
  26.4 4.0 %collective-permute-start.1 = (bf16[64,4,128]{2,1,0:T(4,128)(2,1)S(1)}, bf16[64,4,128]{2,1,0:T(4,128)(2,1)S(1)}, u32[]{:S(2)}, u32[]{:S(2)}) collective-permute-start(bf16[64,4,128]{2,1,0:T(4,128)(2,1)S(1)} %get-tuple-element.9), channel_id=1, source_target_pairs={{0,3},{1,2},{2,1},{3,0},{4,7},{5,6},{6,5},{7,4},{8,11},{9,10},{10,... | collective-permute-start | bytes 196616 | tf_op jit(solution)/shard_map/ppermute | solution.py:270
  27.4 4.0 %collective-permute-start.4 = (f32[2,32]{1,0:T(2,128)S(1)}, f32[2,32]{1,0:T(2,128)S(1)}, u32[]{:S(2)}, u32[]{:S(2)}) collective-permute-start(f32[2,32]{1,0:T(2,128)S(1)} %get-tuple-element.10), channel_id=1, source_target_pairs={{0,9},{1,8},{2,11},{3,10},{4,13},{5,12},{6,15},{7,14},{8,1},{9,0},... | collective-permute-start | bytes 776 | tf_op jit(solution)/shard_map/ppermute | solution.py:270
  30.4 1.3 %collective-permute-start.2 = (bf16[64,4,128]{2,1,0:T(4,128)(2,1)S(1)}, bf16[64,4,128]{2,1,0:T(4,128)(2,1)S(1)}, u32[]{:S(2)}, u32[]{:S(2)}) collective-permute-start(bf16[64,4,128]{2,1,0:T(4,128)(2,1)S(1)} %shard_map.53), channel_id=1, source_target_pairs={{0,1},{1,0},{2,3},{3,2},{4,5},{5,4},{6,7},{7,6},{8,9},{9,8},{10,11... | collective-permute-start | bytes 196616 | tf_op jit(solution)/shard_map/ppermute | solution.py:270

commit v5 on v4

--- a/solution.py
+++ b/solution.py
@@ -11,8 +11,7 @@
 STEPS = 4
 TILE = 8
 SHARED = 2
-CHUNK = 4
-UNROLL = 7
+UNROLL = 8
 
 lam_space = 0.2
 lam_time = 0.08
@@ -35,7 +34,8 @@
         self.plane_rows = rows // planes
         self.own_rows = rows // devices
         self.slab_rows = rows // self.slabs
-        self.window = self.slab_rows + TILE * min(self.slabs - 1, 2)
+        self.window = self.slab_rows + STEPS * min(self.slabs - 1, 2)
+        self.fine = self.dates // TILE
         self.compact = self.slabs == 2 and date_dev == 2
         self.wire = 2 * self.slab_rows + TILE if self.compact else date_dev * self.window
 
@@ -43,7 +43,7 @@
         return index // (self.bands * self.shared)
 
     def start(self, index):
-        first = self.slab(index) * self.slab_rows - TILE
+        first = self.slab(index) * self.slab_rows - STEPS
         last = self.rows - self.window
         if isinstance(index, int):
             return min(max(first, 0), last)
@@ -115,123 +115,170 @@
                 mean = jnp.where(region == g, jnp.broadcast_to(means[date * bands + band][g], (rows, cols)), mean)
             clear = mask_ref[date].astype(jnp.float32)
             anomalies.append(clear * (scenes_ref[date, band].astype(jnp.float32) - mean))
-        for target in range(band, plan.devices, bands):
+        per_slab = bands * plan.shared
+        for slab in range(plan.slabs):
             if plan.compact:
-                slab, size = plan.slab(target), plan.slab_rows
-                for date in range(date_dev):
-                    send_ref[target, date * size : (date + 1) * size] = anomalies[date][
-                        slab * size : (slab + 1) * size
-                    ].astype(jnp.bfloat16)
+                size = plan.slab_rows
+                blocks = [anomaly[slab * size : (slab + 1) * size] for anomaly in anomalies]
                 edge = size if slab == 0 else size - TILE
                 wanted = row < half if slab == 0 else row >= half
-                send_ref[target, 2 * size :] = jnp.where(
-                    wanted,
-                    anomalies[0][edge : edge + TILE],
-                    pltpu.roll(anomalies[1][edge : edge + TILE], half, 0),
-                ).astype(jnp.bfloat16)
+                other = pltpu.roll(anomalies[1][edge : edge + TILE], half, 0)
+                blocks.append(jnp.where(wanted, anomalies[0][edge : edge + TILE], other))
             else:
-                first, size = plan.start(target), plan.window
-                for date in range(date_dev):
-                    send_ref[target, date * size : (date + 1) * size] = anomalies[date][first : first + size].astype(
-                        jnp.bfloat16
-                    )
-
-
-def diffuse_kernel(plan, got_ref, region_ref, gram_ref, field_ref):
-    window, dates, cols = plan.window, plan.dates, got_ref.shape[-1]
+                first = plan.start(slab * per_slab)
+                blocks = [anomaly[first : first + plan.window] for anomaly in anomalies]
+            offset = 0
+            for block in blocks:
+                block = block.astype(jnp.bfloat16)
+                for target in range(slab * per_slab + band, (slab + 1) * per_slab, bands):
+                    send_ref[target, offset : offset + block.shape[0]] = block
+                offset += block.shape[0]
+
+
+def diffuse_kernel(plan, got_ref, region_ref, gram_ref, field_ref, other_ref, wide_ref, land_ref, row_ref, col_ref, turn_ref):
+    window, dates, fine, wire = plan.window, plan.dates, plan.fine, plan.wire
+    cols = got_ref.shape[-1]
     me = lax.axis_index("dates")
     start = plan.start(me)
-    slab_first = plan.slab(me) * plan.slab_rows - start
-    land = (region_ref[pl.ds(pl.multiple_of(start, TILE), window)] > 0).astype(jnp.float32)
+    slab = plan.slab(me)
+    own_first = slab * plan.slab_rows - start
+
+    land_ref[: plan.rows] = (region_ref[...] > 0).astype(jnp.float32)
+    here = land_ref[pl.ds(start, window)]
     row = lax.broadcasted_iota(jnp.int32, (window, cols), 0)
     col = lax.broadcasted_iota(jnp.int32, (window, cols), 1)
-    down = jnp.where(row < window - 1, pltpu.roll(land, window - 1, 0), 0.0)
-    right = jnp.where(col < cols - 1, pltpu.roll(land, cols - 1, 1), 0.0)
-    row_weight = jnp.concatenate([lam_space * land * down] * CHUNK, axis=0)
-    col_weight = jnp.concatenate([lam_space * land * right] * CHUNK, axis=0)
+    above = jnp.where(row > 0, pltpu.roll(here, 1, 0), 0.0)
+    right = jnp.where(col < cols - 1, pltpu.roll(here, cols - 1, 1), 0.0)
+    row_weight = lam_space * here * above
+    col_weight = lam_space * here * right
+    for r in range(window):
+        row_ref[r * TILE : (r + 1) * TILE] = jnp.broadcast_to(row_weight[r : r + 1], (TILE, cols))
+        col_ref[r * TILE : (r + 1) * TILE] = jnp.broadcast_to(col_weight[r : r + 1], (TILE, cols))
+    row_ref[window * TILE :] = jnp.zeros((TILE, cols), jnp.float32)
+    for ref in (field_ref, other_ref):
+        ref[window * dates :] = jnp.zeros((dates, cols), jnp.float32)
+    sublane = lax.broadcasted_iota(jnp.int32, (TILE, cols), 0)
+    last_weight = jnp.where(sublane < TILE - 1, lam_time, 0.0)
     source = lax.broadcasted_iota(jnp.int32, (cols, cols), 0)
     target = lax.broadcasted_iota(jnp.int32, (cols, cols), 1)
     same = (source == target).astype(jnp.float32)
     onward = ((source == target + 1).astype(jnp.float32) - same).astype(jnp.bfloat16)
     inflow = (same - (source + 1 == target).astype(jnp.float32)).astype(jnp.bfloat16)
-    length, chunks = CHUNK * window, dates // CHUNK
-
-    if plan.compact:
-        size, half = plan.slab_rows, TILE // 2
-        edge = jnp.where(slab_first == 0, size, 0)
-        tile_row = lax.broadcasted_iota(jnp.int32, (TILE, cols), 0)
-        wanted = (tile_row < half) == (slab_first == 0)
-        for device in range(plan.devices):
-            halos = got_ref[device, 2 * size :].astype(jnp.float32)
-            for date, halo in enumerate((halos, pltpu.roll(halos, half, 0))):
-                base = (2 * device + date) * window
-                field_ref[pl.ds(pl.multiple_of(base + slab_first, TILE), size)] = got_ref[
-                    device, date * size : (date + 1) * size
-                ].astype(jnp.float32)
-                field_ref[pl.ds(pl.multiple_of(base + edge, TILE), TILE)] = jnp.where(wanted, halo, 0.0)
-    else:
-
-        def unpack(device, carry):
-            field_ref[pl.ds(pl.multiple_of(device * plan.wire, TILE), plan.wire)] = got_ref[device].astype(jnp.float32)
-            return carry
-
-        lax.fori_loop(0, plan.devices, unpack, 0)
+
+    def widen(device, carry):
+        wide_ref[pl.ds(pl.multiple_of(device * wire, TILE), wire)] = got_ref[device].astype(jnp.float32)
+        return carry
+
+    lax.fori_loop(0, plan.devices, widen, 0, unroll=min(plan.devices, 16))
+    old_ref, new_ref = (field_ref, other_ref) if STEPS % 2 == 0 else (other_ref, field_ref)
+    stride = fine // plan.date_dev * wire
+
+    def place(r, first, f):
+        from_row = f // plan.date_dev * wire + first
+        old_ref[pl.ds(pl.multiple_of(r * dates + f * TILE, TILE), TILE)] = wide_ref[pl.ds(from_row, TILE, stride=stride)]
+
+    for f in range(fine):
+        date = f % plan.date_dev
+        if plan.compact:
+            halo = 2 * plan.slab_rows + STEPS * jnp.where(slab == 0, date, 1 - date)
+            halo_row = jnp.where(slab == 0, plan.slab_rows, 0)
+            for i in range(plan.slab_rows):
+                place(own_first + i, date * plan.slab_rows + i, f)
+            for i in range(STEPS):
+                place(halo_row + i, halo + i, f)
+        else:
+            for i in range(window):
+                place(i, date * window + i, f)
+
+    chunk = max(1, 128 // dates)
 
     for step in range(STEPS):
-
-        def read(t):
-            return field_ref[pl.ds(pl.multiple_of(t * window, TILE), length)]
-
-        def advance(current, following, date_in):
+        if plan.compact:
+            base, count = jnp.where(slab == 0, 0, step + 1), window - step - 1
+        else:
+            base, count = 0, window
+
+        def rows(r, n):
+            return pl.ds(pl.multiple_of(r * dates, TILE), n * dates)
+
+        def weights(ref, r, n):
+            parts = []
+            for i in range(n):
+                parts += [ref[pl.ds(pl.multiple_of((r + i) * TILE, TILE), TILE)]] * fine
+            return jnp.concatenate(parts, axis=0)
+
+        def advance(r, n, row_in):
+            current, following = old_ref[rows(r, n)], old_ref[rows(r + 1, n)]
             difference = jnp.dot(current.astype(jnp.bfloat16), onward, preferred_element_type=jnp.float32)
-            col_flux = (col_weight * phi(difference)).astype(jnp.bfloat16)
-            row_flux = row_weight * phi(pltpu.roll(current, length - 1, 0) - current)
-            date_flux = lam_time * phi(following - current)
-            new = (
+            col_flux = (weights(col_ref, r, n) * phi(difference)).astype(jnp.bfloat16)
+            row_flux = weights(row_ref, r + 1, n) * phi(following - current)
+            if n > 1:
+                row_before = jnp.concatenate([row_in, row_flux[:-dates]], axis=0)
+            else:
+                row_before = row_in
+            date_change = []
+            for i in range(n):
+                x = current[i * dates : (i + 1) * dates]
+                later = jnp.concatenate([x[TILE:], pltpu.roll(x[:TILE], TILE - 1, 0)], axis=0)
+                flux = phi(later - x)
+                flux = jnp.concatenate([lam_time * flux[:-TILE], last_weight * flux[-TILE:]], axis=0)
+                date_change.append(flux - jnp.concatenate([pltpu.roll(flux[-TILE:], 1, 0), flux[:-TILE]], axis=0))
+            new_ref[rows(r, n)] = (
                 current
-                + (row_flux - pltpu.roll(row_flux, 1, 0))
+                + (row_flux - row_before)
                 + jnp.dot(col_flux, inflow, preferred_element_type=jnp.float32)
-                + (date_flux - jnp.concatenate([date_in, date_flux[:-window]], axis=0))
+                + (date_change[0] if n == 1 else jnp.concatenate(date_change, axis=0))
             )
-            return new, date_flux[-window:]
-
-        def one(k, date_in):
-            new, date_out = advance(read(k * CHUNK), read(k * CHUNK + 1), date_in)
-            field_ref[pl.ds(pl.multiple_of(k * length, TILE), length)] = new
-            return date_out
-
-        date_in = lax.fori_loop(
-            0, chunks - 1, one, jnp.zeros((window, cols), jnp.float32), unroll=min(chunks - 1, UNROLL)
+            return row_flux[-dates:]
+
+        before = old_ref[rows(jnp.maximum(base - 1, 0), 1)]
+        row_in = weights(row_ref, base, 1) * phi(old_ref[rows(base, 1)] - before)
+        full = count // chunk
+        row_in = lax.fori_loop(
+            0, full, lambda k, carry: advance(base + k * chunk, chunk, carry), row_in, unroll=min(full, UNROLL)
         )
-        current = read((chunks - 1) * CHUNK)
-        new, _ = advance(current, jnp.concatenate([current[window:], current[-window:]], axis=0), date_in)
-        field_ref[pl.ds((chunks - 1) * length, length)] = new
+        if count % chunk:
+            advance(base + full * chunk, count % chunk, row_in)
+        old_ref, new_ref = new_ref, old_ref
 
     def gram_rows(i, total):
-        rows = jnp.concatenate(
-            [field_ref[pl.ds(slab_first + 2 * i + j, dates, stride=window)] for j in range(2)], axis=1
-        ).astype(jnp.bfloat16)
-        return total + lax.dot_general(
-            rows, rows, (((1,), (1,)), ((), ())), preferred_element_type=jnp.float32
-        )
-
-    gram_ref[...] = lax.fori_loop(
+        pair = [
+            field_ref[pl.ds(pl.multiple_of((own_first + 2 * i + j) * dates, TILE), dates)].astype(jnp.bfloat16)
+            for j in range(2)
+        ]
+        both = jnp.concatenate(pair, axis=1)
+        return total + lax.dot_general(both, both, (((1,), (1,)), ((), ())), preferred_element_type=jnp.float32)
+
+    gram = lax.fori_loop(
         0, plan.slab_rows // 2, gram_rows, jnp.zeros((dates, dates), jnp.float32), unroll=min(8, plan.slab_rows // 2)
     )
-
-
-def share_kernel(plan, field_ref, gram_ref, message_ref, rest_ref):
-    window, dates, own = plan.window, plan.dates, plan.own_rows
+    width = turn_ref.shape[1]
+    for last in (False, True):
+        for block in range(dates // width):
+            part = gram[:, block * width : (block + 1) * width]
+            for f in range(fine):
+                turn_ref[pl.ds(block * dates + f, TILE, stride=fine)] = part[f * TILE : (f + 1) * TILE]
+            if last:
+                gram_ref[:, block * width : (block + 1) * width] = turn_ref[block * dates : (block + 1) * dates]
+        if not last:
+            gram = jnp.concatenate(
+                [turn_ref[block * dates : (block + 1) * dates].T for block in range(dates // width)], axis=0
+            )
+
+
+def share_kernel(plan, field_ref, message_ref, rest_ref):
+    dates, fine, own = plan.dates, plan.fine, plan.own_rows
     me = lax.axis_index("dates")
     place = me % plan.bands
     plane_first = (me // plan.bands) * plan.plane_rows - plan.start(me)
 
     def share(t, carry):
+        from_row = t % fine * TILE + t // fine
         for ref, slot, other in (
             (message_ref, t, 3), (message_ref, dates + t, 2), (rest_ref, t, 0), (rest_ref, dates + t, 1)
         ):
-            first = plane_first + (place ^ other) * own
-            ref[slot] = field_ref[pl.ds(t * window + first, own)].astype(jnp.bfloat16)
+            first = (plane_first + (place ^ other) * own) * dates
+            ref[slot] = field_ref[pl.ds(first + from_row, own, stride=dates)].astype(jnp.bfloat16)
         return carry
 
     lax.fori_loop(0, dates, share, 0, unroll=8)
@@ -265,6 +312,10 @@
         copy.wait()
 
 
+def add_kernel(gram_ref, got_ref, message_ref, sum_ref):
+    sum_ref[...] = gram_ref[...] + got_ref[...]
+
+
 def swap(x, bits):
     count = lax.axis_size("dates")
     return lax.ppermute(x, "dates", [(i, i ^ bits) for i in range(count)])
@@ -302,22 +353,37 @@
     got = lax.all_to_all(send, "dates", split_axis=0, concat_axis=0, tiled=True)
     gram, field = pl.pallas_call(
         functools.partial(diffuse_kernel, plan),
-        out_shape=(shape(dates, dates, dtype=jnp.float32), shape(dates * plan.window, cols, dtype=jnp.float32)),
+        out_shape=(shape(dates, dates, dtype=jnp.float32), shape(dates * (plan.window + 1), cols, dtype=jnp.float32)),
         in_specs=[vmem] * 2,
         out_specs=(vmem,) * 2,
+        scratch_shapes=[
+            pltpu.VMEM((dates * (plan.window + 1), cols), jnp.float32),
+            pltpu.VMEM((devices * plan.wire, cols), jnp.float32),
+            pltpu.VMEM((rows, cols), jnp.float32),
+            pltpu.VMEM(((plan.window + 1) * TILE, cols), jnp.float32),
+            pltpu.VMEM((plan.window * TILE, cols), jnp.float32),
+            pltpu.VMEM((dates * max(1, dates // 128), min(dates, 128)), jnp.float32),
+        ],
         compiler_params=params,
     )(got, region)
-    gram = gram + swap(gram, 3)
+    first_gram = swap(gram, 3)
     rows_shape = shape(2 * dates, own, cols)
     message, rest = pl.pallas_call(
         functools.partial(share_kernel, plan),
         out_shape=(rows_shape, rows_shape),
-        in_specs=[vmem] * 2,
+        in_specs=[vmem],
         out_specs=(vmem,) * 2,
         compiler_params=params,
         cost_estimate=small,
-    )(field, gram)
+    )(field)
     first = swap(message, 3)
+    gram = pl.pallas_call(
+        add_kernel,
+        out_shape=shape(dates, dates, dtype=jnp.float32),
+        in_specs=[vmem] * 3,
+        out_specs=vmem,
+        compiler_params=params,
+    )(gram, first_gram, message)
     gram = gram + swap(gram, 1)
 
     bit = bands * plan.shared

time: 32.6 us -> 32.1 us (0.985)
  waiting for transfers between devices: 6.86 us -> 6.48 us
    ppermute x5, waiting for transfers between devices: 6.86 us -> 6.48 us  [swap(): return lax.ppermute(x, 'dates', [(i, i ^ bits) for i in range(count)])]
    pallas_call x1, Pallas kernels: 2.99 us -> 2.61 us  [local(): pl.pallas_call(functools.partial(diffuse_kernel, plan), out_shape=(shape(...]
  transfers between devices with their start and end apart: 5 -> 5, of which waited for: 5 -> 5; matrix products, arithmetic and copies ran while one was open for 0% -> 0% of each run, Pallas kernels for 0% -> 1%
where the time goes in v5:
time: 32.1 us; the launch traced here: 31.8 us
  blocking collectives  17.8 us (55%)
  waiting for transfers between devices  6.48 us (20%)
  Pallas kernels  5.13 us (16%)
  starting transfers between devices  1.78 us (6%)
  between operations  0.67 us (2%)
    all_to_all x1, blocking collectives, local(): got = lax.all_to_all(send, 'dates', split_axis=0, concat_axis=0, tiled=True)  17.8 us
    ppermute x5, waiting for transfers between devices, swap(): return lax.ppermute(x, 'dates', [(i, i ^ bits) for i in range(count)])  6.48 us
    pallas_call x1, Pallas kernels, local(): pl.pallas_call(functools.partial(diffuse_kernel, plan), out_shape=(shape(...  2.61 us
    ppermute x5, starting transfers between devices, swap(): return lax.ppermute(x, 'dates', [(i, i ^ bits) for i in range(count)])  1.78 us
    pallas_call x1, Pallas kernels, local(): pl.pallas_call(functools.partial(anomaly_kernel, plan), out_shape=shape(d...  1.49 us
    pallas_call x1, Pallas kernels, local(): pl.pallas_call(functools.partial(finish_kernel, plan), out_shape=(shape(d...  0.69 us
  transfers between devices with their start and end apart: 5, of which 5 were waited for; matrix products, arithmetic and copies ran while one was open for 0% of the time, Pallas kernels for 1%

profile of v5, /device:TPU:0, one launch (start us, length us, event | category | flops | bytes accessed | tf_op | source)
XLA Modules:
  0.0 31.8 jit_solution(12612127240660054678)
XLA Ops:
  0.6 1.5 %shard_map.50 = bf16[16,72,128]{2,1,0:T(8,128)(2,1)S(1)} custom-call(bf16[2,4,64,128]{3,2,1,0:T(8,128)(2,1)} %scenes_hbm.1, s32[2,64,128]{2,1,0:T(8,128)} %mask_hbm.1, s32[64,128]{1,0:T(8,128)} %region_ref.1), custom_call_target="tpu_custom_call" | custom-call | tf_op jit(solution)/shard_map/pallas_call | solution.py:339
  2.1 0.0 copy-start
  2.1 17.8 %all_to_all.5.got_ref = bf16[16,72,128]{2,1,0:T(8,128)(2,1)S(1)} all-to-all(bf16[16,72,128]{2,1,0:T(8,128)(2,1)S(1)} %shard_map.50), channel_id=1, replica_groups=mesh['groups'=2,'dates'=16] {'dates'}, dimensions={0} | all-to-all | bytes 589824 | tf_op jit(solution)/shard_map/all_to_all | solution.py:353
  19.9 0.0 copy-done
  19.9 2.6 %shard_map.51 = (f32[32,32]{1,0:T(8,128)S(1)}, f32[1184,128]{1,0:T(8,128)S(1)}) custom-call(bf16[16,72,128]{2,1,0:T(8,128)(2,1)S(1)} %all_to_all.5.got_ref, s32[64,128]{1,0:T(8,128)S(1)} %copy-done), custom_call_target="tpu_custom_call" | custom-call | tf_op jit(solution)/shard_map/pallas_call | solution.py:354
  22.5 0.3 collective-permute-start.2
  22.8 0.3 %shard_map.52 = (bf16[64,4,128]{2,1,0:T(4,128)(2,1)S(1)}, bf16[64,4,128]{2,1,0:T(4,128)(2,1)S(1)}) custom-call(f32[1184,128]{1,0:T(8,128)S(1)} %get-tuple-element.6.field_ref), custom_call_target="tpu_custom_call" | custom-call | flops 65536 | bytes 262144 | tf_op jit(solution)/shard_map/pallas_call | solution.py:371
  23.1 2.7 %collective-permute-done.2.got_ref = f32[32,32]{1,0:T(8,128)S(1)} collective-permute-done((f32[32,32]{1,0:T(8,128)S(1)}, f32[32,32]{1,0:T(8,128)S(1)}, u32[]{:S(2)}, u32[]{:S(2)}) %collective-permute-start.2) | collective-permute-done | bytes 4128 | tf_op jit(solution)/shard_map/ppermute | solution.py:321
  25.8 0.1 collective-permute-start.3
  25.9 0.1 collective-permute-start
  26.0 0.9 %collective-permute-done.3 = f32[32,32]{1,0:T(8,128)S(1)} collective-permute-done((f32[32,32]{1,0:T(8,128)S(1)}, f32[32,32]{1,0:T(8,128)S(1)}, u32[]{:S(2)}, u32[]{:S(2)}) %collective-permute-start.3) | collective-permute-done | bytes 4128 | tf_op jit(solution)/shard_map/ppermute | solution.py:321
  27.0 1.0 %collective-permute-start.4 = (f32[2,32]{1,0:T(2,128)S(1)}, f32[2,32]{1,0:T(2,128)S(1)}, u32[]{:S(2)}, u32[]{:S(2)}) collective-permute-start(f32[2,32]{1,0:T(2,128)S(1)} %get-tuple-element.10), channel_id=1, source_target_pairs={{0,9},{1,8},{2,11},{3,10},{4,13},{5,12},{6,15},{7,14},{8,1},{9,0},... | collective-permute-start | bytes 776 | tf_op jit(solution)/shard_map/ppermute | solution.py:321
  28.0 1.9 %collective-permute-done.got_ref.first_ref = bf16[64,4,128]{2,1,0:T(4,128)(2,1)S(1)} collective-permute-done((bf16[64,4,128]{2,1,0:T(4,128)(2,1)S(1)}, bf16[64,4,128]{2,1,0:T(4,128)(2,1)S(1)}, u32[]{:S(2)}, u32[]{:S(2)}) %collective-permute-start) | collective-permute-done | bytes 65568 | tf_op jit(solution)/shard_map/ppermute | solution.py:321
  29.9 0.3 collective-permute-start.1
  30.2 0.8 %collective-permute-done.4.other_ref = f32[2,32]{1,0:T(2,128)S(1)} collective-permute-done((f32[2,32]{1,0:T(2,128)S(1)}, f32[2,32]{1,0:T(2,128)S(1)}, u32[]{:S(2)}, u32[]{:S(2)}) %collective-permute-start.4) | collective-permute-done | bytes 288 | tf_op jit(solution)/shard_map/ppermute | solution.py:321
  31.0 0.2 collective-permute-done.1.second_ref
  31.1 0.7 %shard_map.56 = (bf16[32,4,4,128]{3,2,1,0:T(4,128)(2,1)}, f32[2,32]{1,0:T(2,128)}) custom-call(bf16[64,4,128]{2,1,0:T(4,128)(2,1)S(1)} %get-tuple-element.7.rest_ref, bf16[64,4,128]{2,1,0:T(4,128)(2,1)S(1)} %collective-permute-done.got_ref.first_ref, bf16[64,4,128]{2,1,0:T(4,128)(2,1)S(1)} %collective-permute-done.1.second_ref, f32[2,32]{1,0:T(2,128)S(1)} %shard_map.55.sim_ref), custom_call_target="tpu_custom_call" | custom-call | flops 65536 | bytes 262144 | tf_op jit(solution)/shard_map/pallas_call | solution.py:416
  (5 shorter events, 0.0 us)
Async XLA Ops:
  2.1 17.8 %copy-start = (s32[64,128]{1,0:T(8,128)S(1)}, s32[64,128]{1,0:T(8,128)}, u32[]{:S(2)}) copy-start(s32[64,128]{1,0:T(8,128)} %region_ref.1) | copy-start | bytes 98308
  22.5 3.3 %collective-permute-start.2 = (f32[32,32]{1,0:T(8,128)S(1)}, f32[32,32]{1,0:T(8,128)S(1)}, u32[]{:S(2)}, u32[]{:S(2)}) collective-permute-start(f32[32,32]{1,0:T(8,128)S(1)} %get-tuple-element.9.gram_ref), channel_id=1, source_target_pairs={{0,3},{1,2},{2,1},{3,0},{4,7},{5,6},{6,5},{7,4},{8,11},{9,10},{10,... | collective-permute-start | bytes 12296 | tf_op jit(solution)/shard_map/ppermute | solution.py:321
  25.8 1.2 %collective-permute-start.3 = (f32[32,32]{1,0:T(8,128)S(1)}, f32[32,32]{1,0:T(8,128)S(1)}, u32[]{:S(2)}, u32[]{:S(2)}) collective-permute-start(f32[32,32]{1,0:T(8,128)S(1)} %shard_map.54), channel_id=1, source_target_pairs={{0,1},{1,0},{2,3},{3,2},{4,5},{5,4},{6,7},{7,6},{8,9},{9,8},{10,11... | collective-permute-start | bytes 12296 | tf_op jit(solution)/shard_map/ppermute | solution.py:321
  25.9 3.9 %collective-permute-start = (bf16[64,4,128]{2,1,0:T(4,128)(2,1)S(1)}, bf16[64,4,128]{2,1,0:T(4,128)(2,1)S(1)}, u32[]{:S(2)}, u32[]{:S(2)}) collective-permute-start(bf16[64,4,128]{2,1,0:T(4,128)(2,1)S(1)} %get-tuple-element.8.message_ref), channel_id=1, source_target_pairs={{0,3},{1,2},{2,1},{3,0},{4,7},{5,6},{6,5},{7,4},{8,11},{9,10},{10,... | collective-permute-start | bytes 196616 | tf_op jit(solution)/shard_map/ppermute | solution.py:321
  27.0 4.0 %collective-permute-start.4 = (f32[2,32]{1,0:T(2,128)S(1)}, f32[2,32]{1,0:T(2,128)S(1)}, u32[]{:S(2)}, u32[]{:S(2)}) collective-permute-start(f32[2,32]{1,0:T(2,128)S(1)} %get-tuple-element.10), channel_id=1, source_target_pairs={{0,9},{1,8},{2,11},{3,10},{4,13},{5,12},{6,15},{7,14},{8,1},{9,0},... | collective-permute-start | bytes 776 | tf_op jit(solution)/shard_map/ppermute | solution.py:321
  29.9 1.3 %collective-permute-start.1 = (bf16[64,4,128]{2,1,0:T(4,128)(2,1)S(1)}, bf16[64,4,128]{2,1,0:T(4,128)(2,1)S(1)}, u32[]{:S(2)}, u32[]{:S(2)}) collective-permute-start(bf16[64,4,128]{2,1,0:T(4,128)(2,1)S(1)} %shard_map.53), channel_id=1, source_target_pairs={{0,1},{1,0},{2,3},{3,2},{4,5},{5,4},{6,7},{7,6},{8,9},{9,8},{10,11... | collective-permute-start | bytes 196616 | tf_op jit(solution)/shard_map/ppermute | solution.py:321

commit v6 on v5

--- a/solution.py
+++ b/solution.py
@@ -80,11 +80,9 @@
             label = jnp.where(clear, region_ref[tile_rows(i)], -1)
             values = [scenes_ref[date, band, tile_rows(i)].astype(jnp.float32) for band in range(bands)]
             out = []
-            for g in range(REGIONS):
-                here = label == g
-                for band in range(bands):
-                    out.append(sums[g * per_region + band] + fold(jnp.where(here, values[band], 0.0)))
-                out.append(sums[g * per_region + bands] + fold(jnp.where(here, 1.0, 0.0)))
+            here = [label == g for g in range(REGIONS)]
+            for value in (*values, 1.0):
+                out += [sums[len(out) + g] + fold(jnp.where(here[g], value, 0.0)) for g in range(REGIONS)]
             return tuple(out)
 
         zero = jnp.zeros((TILE, cols), jnp.float32)
@@ -95,14 +93,10 @@
     means = []
     for date in range(date_dev):
         totals = jnp.sum(sums_ref[date], axis=1, keepdims=True)
+        counts = totals[bands * REGIONS :] + 1.0
         for band in range(bands):
-            means.append(
-                [
-                    totals[g * per_region + band : g * per_region + band + 1]
-                    / (totals[g * per_region + bands : g * per_region + bands + 1] + 1.0)
-                    for g in range(REGIONS)
-                ]
-            )
+            mean = totals[band * REGIONS : (band + 1) * REGIONS] / counts
+            means.append([mean[g : g + 1] for g in range(REGIONS)])
 
     region = region_ref[...]
     row = lax.broadcasted_iota(jnp.int32, (TILE, cols), 0)
@@ -366,7 +360,7 @@
         ],
         compiler_params=params,
     )(got, region)
-    first_gram = swap(gram, 3)
+    first_gram = swap(gram, 1)
     rows_shape = shape(2 * dates, own, cols)
     message, rest = pl.pallas_call(
         functools.partial(share_kernel, plan),
@@ -384,7 +378,7 @@
         out_specs=vmem,
         compiler_params=params,
     )(gram, first_gram, message)
-    gram = gram + swap(gram, 1)
+    gram = gram + swap(gram, 3)
 
     bit = bands * plan.shared
     while 2 * bit < devices:

time: 32.1 us -> 32 us (level)
  waiting for transfers between devices: 6.48 us -> 4.56 us
  starting transfers between devices: 1.78 us -> 3.38 us
    ppermute x5, waiting for transfers between devices: 6.48 us -> 4.56 us  [swap(): return lax.ppermute(x, 'dates', [(i, i ^ bits) for i in range(count)])]
    ppermute x5, starting transfers between devices: 1.78 us -> 3.38 us  [swap(): return lax.ppermute(x, 'dates', [(i, i ^ bits) for i in range(count)])]
  transfers between devices with their start and end apart: 5 -> 5, of which waited for: 5 -> 3; matrix products, arithmetic and copies ran while one was open for 0% -> 0% of each run, Pallas kernels for 1% -> 1%
where the time goes in v6:
time: 32 us; the launch traced here: 31.6 us
  blocking collectives  17.8 us (56%)
  Pallas kernels  5.16 us (16%)
  waiting for transfers between devices  4.56 us (14%)
  starting transfers between devices  3.38 us (11%)
  between operations  0.68 us (2%)
    all_to_all x1, blocking collectives, local(): got = lax.all_to_all(send, 'dates', split_axis=0, concat_axis=0, tiled=True)  17.8 us
    ppermute x5, waiting for transfers between devices, swap(): return lax.ppermute(x, 'dates', [(i, i ^ bits) for i in range(count)])  4.56 us
    ppermute x5, starting transfers between devices, swap(): return lax.ppermute(x, 'dates', [(i, i ^ bits) for i in range(count)])  3.38 us
    pallas_call x1, Pallas kernels, local(): pl.pallas_call(functools.partial(diffuse_kernel, plan), out_shape=(shape(...  2.61 us
    pallas_call x1, Pallas kernels, local(): pl.pallas_call(functools.partial(anomaly_kernel, plan), out_shape=shape(d...  1.47 us
    pallas_call x1, Pallas kernels, local(): pl.pallas_call(functools.partial(finish_kernel, plan), out_shape=(shape(d...  0.7 us
  transfers between devices with their start and end apart: 5, of which 3 were waited for; matrix products, arithmetic and copies ran while one was open for 0% of the time, Pallas kernels for 1%

profile of v6, /device:TPU:0, one launch (start us, length us, event | category | flops | bytes accessed | tf_op | source)
XLA Modules:
  0.0 31.6 jit_solution(14786885074684326913)
XLA Ops:
  0.6 1.5 %shard_map.50 = bf16[16,72,128]{2,1,0:T(8,128)(2,1)S(1)} custom-call(bf16[2,4,64,128]{3,2,1,0:T(8,128)(2,1)} %scenes_hbm.1, s32[2,64,128]{2,1,0:T(8,128)} %mask_hbm.1, s32[64,128]{1,0:T(8,128)} %region_ref.1), custom_call_target="tpu_custom_call" | custom-call | tf_op jit(solution)/shard_map/pallas_call | solution.py:333
  2.1 0.0 copy-start
  2.1 17.8 %all_to_all.5.got_ref = bf16[16,72,128]{2,1,0:T(8,128)(2,1)S(1)} all-to-all(bf16[16,72,128]{2,1,0:T(8,128)(2,1)S(1)} %shard_map.50), channel_id=1, replica_groups=mesh['groups'=2,'dates'=16] {'dates'}, dimensions={0} | all-to-all | bytes 589824 | tf_op jit(solution)/shard_map/all_to_all | solution.py:347
  19.9 0.0 copy-done
  19.9 2.6 %shard_map.51 = (f32[32,32]{1,0:T(8,128)S(1)}, f32[1184,128]{1,0:T(8,128)S(1)}) custom-call(bf16[16,72,128]{2,1,0:T(8,128)(2,1)S(1)} %all_to_all.5.got_ref, s32[64,128]{1,0:T(8,128)S(1)} %copy-done), custom_call_target="tpu_custom_call" | custom-call | tf_op jit(solution)/shard_map/pallas_call | solution.py:348
  22.5 0.0 collective-permute-start.2
  22.5 0.4 %shard_map.52 = (bf16[64,4,128]{2,1,0:T(4,128)(2,1)S(1)}, bf16[64,4,128]{2,1,0:T(4,128)(2,1)S(1)}) custom-call(f32[1184,128]{1,0:T(8,128)S(1)} %get-tuple-element.6.field_ref), custom_call_target="tpu_custom_call" | custom-call | flops 65536 | bytes 262144 | tf_op jit(solution)/shard_map/pallas_call | solution.py:365
  22.9 0.8 %collective-permute-done.2.got_ref = f32[32,32]{1,0:T(8,128)S(1)} collective-permute-done((f32[32,32]{1,0:T(8,128)S(1)}, f32[32,32]{1,0:T(8,128)S(1)}, u32[]{:S(2)}, u32[]{:S(2)}) %collective-permute-start.2) | collective-permute-done | bytes 4128 | tf_op jit(solution)/shard_map/ppermute | solution.py:315
  23.7 0.3 collective-permute-start.3
  24.0 1.5 %collective-permute-start = (bf16[64,4,128]{2,1,0:T(4,128)(2,1)S(1)}, bf16[64,4,128]{2,1,0:T(4,128)(2,1)S(1)}, u32[]{:S(2)}, u32[]{:S(2)}) collective-permute-start(bf16[64,4,128]{2,1,0:T(4,128)(2,1)S(1)} %get-tuple-element.8.message_ref), channel_id=1, source_target_pairs={{0,3},{1,2},{2,1},{3,0},{4,7},{5,6},{6,5},{7,4},{8,11},{9,10},{10,... | collective-permute-start | bytes 196616 | tf_op jit(solution)/shard_map/ppermute | solution.py:315
  25.5 1.4 %collective-permute-done.3 = f32[32,32]{1,0:T(8,128)S(1)} collective-permute-done((f32[32,32]{1,0:T(8,128)S(1)}, f32[32,32]{1,0:T(8,128)S(1)}, u32[]{:S(2)}, u32[]{:S(2)}) %collective-permute-start.3) | collective-permute-done | bytes 4128 | tf_op jit(solution)/shard_map/ppermute | solution.py:315
  26.9 1.5 %collective-permute-start.4 = (f32[2,32]{1,0:T(2,128)S(1)}, f32[2,32]{1,0:T(2,128)S(1)}, u32[]{:S(2)}, u32[]{:S(2)}) collective-permute-start(f32[2,32]{1,0:T(2,128)S(1)} %get-tuple-element.10), channel_id=1, source_target_pairs={{0,9},{1,8},{2,11},{3,10},{4,13},{5,12},{6,15},{7,14},{8,1},{9,0},... | collective-permute-start | bytes 776 | tf_op jit(solution)/shard_map/ppermute | solution.py:315
  28.4 0.0 collective-permute-done.got_ref.first_ref
  28.4 0.1 collective-permute-start.1
  28.5 2.3 %collective-permute-done.4.other_ref = f32[2,32]{1,0:T(2,128)S(1)} collective-permute-done((f32[2,32]{1,0:T(2,128)S(1)}, f32[2,32]{1,0:T(2,128)S(1)}, u32[]{:S(2)}, u32[]{:S(2)}) %collective-permute-start.4) | collective-permute-done | bytes 288 | tf_op jit(solution)/shard_map/ppermute | solution.py:315
  30.8 0.0 collective-permute-done.1.second_ref
  30.9 0.7 %shard_map.56 = (bf16[32,4,4,128]{3,2,1,0:T(4,128)(2,1)}, f32[2,32]{1,0:T(2,128)}) custom-call(bf16[64,4,128]{2,1,0:T(4,128)(2,1)S(1)} %get-tuple-element.7.rest_ref, bf16[64,4,128]{2,1,0:T(4,128)(2,1)S(1)} %collective-permute-done.got_ref.first_ref, bf16[64,4,128]{2,1,0:T(4,128)(2,1)S(1)} %collective-permute-done.1.second_ref, f32[2,32]{1,0:T(2,128)S(1)} %shard_map.55.sim_ref), custom_call_target="tpu_custom_call" | custom-call | flops 65536 | bytes 262144 | tf_op jit(solution)/shard_map/pallas_call | solution.py:410
  (5 shorter events, 0.0 us)
Async XLA Ops:
  2.1 17.8 %copy-start = (s32[64,128]{1,0:T(8,128)S(1)}, s32[64,128]{1,0:T(8,128)}, u32[]{:S(2)}) copy-start(s32[64,128]{1,0:T(8,128)} %region_ref.1) | copy-start | bytes 98308
  22.5 1.2 %collective-permute-start.2 = (f32[32,32]{1,0:T(8,128)S(1)}, f32[32,32]{1,0:T(8,128)S(1)}, u32[]{:S(2)}, u32[]{:S(2)}) collective-permute-start(f32[32,32]{1,0:T(8,128)S(1)} %get-tuple-element.9.gram_ref), channel_id=1, source_target_pairs={{0,1},{1,0},{2,3},{3,2},{4,5},{5,4},{6,7},{7,6},{8,9},{9,8},{10,11... | collective-permute-start | bytes 12296 | tf_op jit(solution)/shard_map/ppermute | solution.py:315
  23.7 3.2 %collective-permute-start.3 = (f32[32,32]{1,0:T(8,128)S(1)}, f32[32,32]{1,0:T(8,128)S(1)}, u32[]{:S(2)}, u32[]{:S(2)}) collective-permute-start(f32[32,32]{1,0:T(8,128)S(1)} %shard_map.54), channel_id=1, source_target_pairs={{0,3},{1,2},{2,1},{3,0},{4,7},{5,6},{6,5},{7,4},{8,11},{9,10},{10,... | collective-permute-start | bytes 12296 | tf_op jit(solution)/shard_map/ppermute | solution.py:315
  24.0 4.5 %collective-permute-start = (bf16[64,4,128]{2,1,0:T(4,128)(2,1)S(1)}, bf16[64,4,128]{2,1,0:T(4,128)(2,1)S(1)}, u32[]{:S(2)}, u32[]{:S(2)}) collective-permute-start(bf16[64,4,128]{2,1,0:T(4,128)(2,1)S(1)} %get-tuple-element.8.message_ref), channel_id=1, source_target_pairs={{0,3},{1,2},{2,1},{3,0},{4,7},{5,6},{6,5},{7,4},{8,11},{9,10},{10,... | collective-permute-start | bytes 196616 | tf_op jit(solution)/shard_map/ppermute | solution.py:315
  26.9 4.0 %collective-permute-start.4 = (f32[2,32]{1,0:T(2,128)S(1)}, f32[2,32]{1,0:T(2,128)S(1)}, u32[]{:S(2)}, u32[]{:S(2)}) collective-permute-start(f32[2,32]{1,0:T(2,128)S(1)} %get-tuple-element.10), channel_id=1, source_target_pairs={{0,9},{1,8},{2,11},{3,10},{4,13},{5,12},{6,15},{7,14},{8,1},{9,0},... | collective-permute-start | bytes 776 | tf_op jit(solution)/shard_map/ppermute | solution.py:315
  28.4 2.4 %collective-permute-start.1 = (bf16[64,4,128]{2,1,0:T(4,128)(2,1)S(1)}, bf16[64,4,128]{2,1,0:T(4,128)(2,1)S(1)}, u32[]{:S(2)}, u32[]{:S(2)}) collective-permute-start(bf16[64,4,128]{2,1,0:T(4,128)(2,1)S(1)} %shard_map.53), channel_id=1, source_target_pairs={{0,1},{1,0},{2,3},{3,2},{4,5},{5,4},{6,7},{7,6},{8,9},{9,8},{10,11... | collective-permute-start | bytes 196616 | tf_op jit(solution)/shard_map/ppermute | solution.py:315

commit v7 on v6

--- a/solution.py
+++ b/solution.py
@@ -12,6 +12,7 @@
 TILE = 8
 SHARED = 2
 UNROLL = 8
+GRAM_ROWS = 4
 
 lam_space = 0.2
 lam_time = 0.08
@@ -184,7 +185,7 @@
             for i in range(window):
                 place(i, date * window + i, f)
 
-    chunk = max(1, 128 // dates)
+    chunk = max(1, 256 // dates)
 
     for step in range(STEPS):
         if plan.compact:
@@ -237,14 +238,14 @@
 
     def gram_rows(i, total):
         pair = [
-            field_ref[pl.ds(pl.multiple_of((own_first + 2 * i + j) * dates, TILE), dates)].astype(jnp.bfloat16)
-            for j in range(2)
+            field_ref[pl.ds(pl.multiple_of((own_first + GRAM_ROWS * i + j) * dates, TILE), dates)].astype(jnp.bfloat16)
+            for j in range(GRAM_ROWS)
         ]
         both = jnp.concatenate(pair, axis=1)
         return total + lax.dot_general(both, both, (((1,), (1,)), ((), ())), preferred_element_type=jnp.float32)
 
     gram = lax.fori_loop(
-        0, plan.slab_rows // 2, gram_rows, jnp.zeros((dates, dates), jnp.float32), unroll=min(8, plan.slab_rows // 2)
+        0, plan.slab_rows // GRAM_ROWS, gram_rows, jnp.zeros((dates, dates), jnp.float32), unroll=min(8, plan.slab_rows // GRAM_ROWS)
     )
     width = turn_ref.shape[1]
     for last in (False, True):

time: 32 us -> 32 us (level)
  no operation moved by 1% of the time
where the time goes in v7:
time: 32 us; the launch traced here: 31.6 us
  blocking collectives  17.8 us (56%)
  Pallas kernels  5.17 us (16%)
  waiting for transfers between devices  4.56 us (14%)
  starting transfers between devices  3.4 us (11%)
  between operations  0.68 us (2%)
    all_to_all x1, blocking collectives, local(): got = lax.all_to_all(send, 'dates', split_axis=0, concat_axis=0, tiled=True)  17.8 us
    ppermute x5, waiting for transfers between devices, swap(): return lax.ppermute(x, 'dates', [(i, i ^ bits) for i in range(count)])  4.56 us
    ppermute x5, starting transfers between devices, swap(): return lax.ppermute(x, 'dates', [(i, i ^ bits) for i in range(count)])  3.4 us
    pallas_call x1, Pallas kernels, local(): pl.pallas_call(functools.partial(diffuse_kernel, plan), out_shape=(shape(...  2.62 us
    pallas_call x1, Pallas kernels, local(): pl.pallas_call(functools.partial(anomaly_kernel, plan), out_shape=shape(d...  1.47 us
    pallas_call x1, Pallas kernels, local(): pl.pallas_call(functools.partial(finish_kernel, plan), out_shape=(shape(d...  0.7 us
  transfers between devices with their start and end apart: 5, of which 3 were waited for; matrix products, arithmetic and copies ran while one was open for 0% of the time, Pallas kernels for 1%

profile of v7, /device:TPU:0, one launch (start us, length us, event | category | flops | bytes accessed | tf_op | source)
XLA Modules:
  0.0 31.6 jit_solution(16043659552541429966)
XLA Ops:
  0.6 1.5 %shard_map.50 = bf16[16,72,128]{2,1,0:T(8,128)(2,1)S(1)} custom-call(bf16[2,4,64,128]{3,2,1,0:T(8,128)(2,1)} %scenes_hbm.1, s32[2,64,128]{2,1,0:T(8,128)} %mask_hbm.1, s32[64,128]{1,0:T(8,128)} %region_ref.1), custom_call_target="tpu_custom_call" | custom-call | tf_op jit(solution)/shard_map/pallas_call | solution.py:334
  2.1 0.0 copy-start
  2.1 17.8 %all_to_all.5.got_ref = bf16[16,72,128]{2,1,0:T(8,128)(2,1)S(1)} all-to-all(bf16[16,72,128]{2,1,0:T(8,128)(2,1)S(1)} %shard_map.50), channel_id=1, replica_groups=mesh['groups'=2,'dates'=16] {'dates'}, dimensions={0} | all-to-all | bytes 589824 | tf_op jit(solution)/shard_map/all_to_all | solution.py:348
  19.9 0.0 copy-done
  19.9 2.6 %shard_map.51 = (f32[32,32]{1,0:T(8,128)S(1)}, f32[1184,128]{1,0:T(8,128)S(1)}) custom-call(bf16[16,72,128]{2,1,0:T(8,128)(2,1)S(1)} %all_to_all.5.got_ref, s32[64,128]{1,0:T(8,128)S(1)} %copy-done), custom_call_target="tpu_custom_call" | custom-call | tf_op jit(solution)/shard_map/pallas_call | solution.py:349
  22.5 0.0 collective-permute-start.2
  22.6 0.4 %shard_map.52 = (bf16[64,4,128]{2,1,0:T(4,128)(2,1)S(1)}, bf16[64,4,128]{2,1,0:T(4,128)(2,1)S(1)}) custom-call(f32[1184,128]{1,0:T(8,128)S(1)} %get-tuple-element.6.field_ref), custom_call_target="tpu_custom_call" | custom-call | flops 65536 | bytes 262144 | tf_op jit(solution)/shard_map/pallas_call | solution.py:366
  22.9 0.8 %collective-permute-done.2.got_ref = f32[32,32]{1,0:T(8,128)S(1)} collective-permute-done((f32[32,32]{1,0:T(8,128)S(1)}, f32[32,32]{1,0:T(8,128)S(1)}, u32[]{:S(2)}, u32[]{:S(2)}) %collective-permute-start.2) | collective-permute-done | bytes 4128 | tf_op jit(solution)/shard_map/ppermute | solution.py:316
  23.7 0.3 collective-permute-start.3
  24.0 1.5 %collective-permute-start = (bf16[64,4,128]{2,1,0:T(4,128)(2,1)S(1)}, bf16[64,4,128]{2,1,0:T(4,128)(2,1)S(1)}, u32[]{:S(2)}, u32[]{:S(2)}) collective-permute-start(bf16[64,4,128]{2,1,0:T(4,128)(2,1)S(1)} %get-tuple-element.8.message_ref), channel_id=1, source_target_pairs={{0,3},{1,2},{2,1},{3,0},{4,7},{5,6},{6,5},{7,4},{8,11},{9,10},{10,... | collective-permute-start | bytes 196616 | tf_op jit(solution)/shard_map/ppermute | solution.py:316
  25.5 1.4 %collective-permute-done.3 = f32[32,32]{1,0:T(8,128)S(1)} collective-permute-done((f32[32,32]{1,0:T(8,128)S(1)}, f32[32,32]{1,0:T(8,128)S(1)}, u32[]{:S(2)}, u32[]{:S(2)}) %collective-permute-start.3) | collective-permute-done | bytes 4128 | tf_op jit(solution)/shard_map/ppermute | solution.py:316
  26.9 1.5 %collective-permute-start.4 = (f32[2,32]{1,0:T(2,128)S(1)}, f32[2,32]{1,0:T(2,128)S(1)}, u32[]{:S(2)}, u32[]{:S(2)}) collective-permute-start(f32[2,32]{1,0:T(2,128)S(1)} %get-tuple-element.10), channel_id=1, source_target_pairs={{0,9},{1,8},{2,11},{3,10},{4,13},{5,12},{6,15},{7,14},{8,1},{9,0},... | collective-permute-start | bytes 776 | tf_op jit(solution)/shard_map/ppermute | solution.py:316
  28.5 0.0 collective-permute-done.got_ref.first_ref
  28.5 0.1 collective-permute-start.1
  28.6 2.3 %collective-permute-done.4.other_ref = f32[2,32]{1,0:T(2,128)S(1)} collective-permute-done((f32[2,32]{1,0:T(2,128)S(1)}, f32[2,32]{1,0:T(2,128)S(1)}, u32[]{:S(2)}, u32[]{:S(2)}) %collective-permute-start.4) | collective-permute-done | bytes 288 | tf_op jit(solution)/shard_map/ppermute | solution.py:316
  30.9 0.0 collective-permute-done.1.second_ref
  30.9 0.7 %shard_map.56 = (bf16[32,4,4,128]{3,2,1,0:T(4,128)(2,1)}, f32[2,32]{1,0:T(2,128)}) custom-call(bf16[64,4,128]{2,1,0:T(4,128)(2,1)S(1)} %get-tuple-element.7.rest_ref, bf16[64,4,128]{2,1,0:T(4,128)(2,1)S(1)} %collective-permute-done.got_ref.first_ref, bf16[64,4,128]{2,1,0:T(4,128)(2,1)S(1)} %collective-permute-done.1.second_ref, f32[2,32]{1,0:T(2,128)S(1)} %shard_map.55.sim_ref), custom_call_target="tpu_custom_call" | custom-call | flops 65536 | bytes 262144 | tf_op jit(solution)/shard_map/pallas_call | solution.py:411
  (5 shorter events, 0.0 us)
Async XLA Ops:
  2.1 17.8 %copy-start = (s32[64,128]{1,0:T(8,128)S(1)}, s32[64,128]{1,0:T(8,128)}, u32[]{:S(2)}) copy-start(s32[64,128]{1,0:T(8,128)} %region_ref.1) | copy-start | bytes 98308
  22.5 1.2 %collective-permute-start.2 = (f32[32,32]{1,0:T(8,128)S(1)}, f32[32,32]{1,0:T(8,128)S(1)}, u32[]{:S(2)}, u32[]{:S(2)}) collective-permute-start(f32[32,32]{1,0:T(8,128)S(1)} %get-tuple-element.9.gram_ref), channel_id=1, source_target_pairs={{0,1},{1,0},{2,3},{3,2},{4,5},{5,4},{6,7},{7,6},{8,9},{9,8},{10,11... | collective-permute-start | bytes 12296 | tf_op jit(solution)/shard_map/ppermute | solution.py:316
  23.7 3.2 %collective-permute-start.3 = (f32[32,32]{1,0:T(8,128)S(1)}, f32[32,32]{1,0:T(8,128)S(1)}, u32[]{:S(2)}, u32[]{:S(2)}) collective-permute-start(f32[32,32]{1,0:T(8,128)S(1)} %shard_map.54), channel_id=1, source_target_pairs={{0,3},{1,2},{2,1},{3,0},{4,7},{5,6},{6,5},{7,4},{8,11},{9,10},{10,... | collective-permute-start | bytes 12296 | tf_op jit(solution)/shard_map/ppermute | solution.py:316
  24.0 4.5 %collective-permute-start = (bf16[64,4,128]{2,1,0:T(4,128)(2,1)S(1)}, bf16[64,4,128]{2,1,0:T(4,128)(2,1)S(1)}, u32[]{:S(2)}, u32[]{:S(2)}) collective-permute-start(bf16[64,4,128]{2,1,0:T(4,128)(2,1)S(1)} %get-tuple-element.8.message_ref), channel_id=1, source_target_pairs={{0,3},{1,2},{2,1},{3,0},{4,7},{5,6},{6,5},{7,4},{8,11},{9,10},{10,... | collective-permute-start | bytes 196616 | tf_op jit(solution)/shard_map/ppermute | solution.py:316
  26.9 4.0 %collective-permute-start.4 = (f32[2,32]{1,0:T(2,128)S(1)}, f32[2,32]{1,0:T(2,128)S(1)}, u32[]{:S(2)}, u32[]{:S(2)}) collective-permute-start(f32[2,32]{1,0:T(2,128)S(1)} %get-tuple-element.10), channel_id=1, source_target_pairs={{0,9},{1,8},{2,11},{3,10},{4,13},{5,12},{6,15},{7,14},{8,1},{9,0},... | collective-permute-start | bytes 776 | tf_op jit(solution)/shard_map/ppermute | solution.py:316
  28.5 2.4 %collective-permute-start.1 = (bf16[64,4,128]{2,1,0:T(4,128)(2,1)S(1)}, bf16[64,4,128]{2,1,0:T(4,128)(2,1)S(1)}, u32[]{:S(2)}, u32[]{:S(2)}) collective-permute-start(bf16[64,4,128]{2,1,0:T(4,128)(2,1)S(1)} %shard_map.53), channel_id=1, source_target_pairs={{0,1},{1,0},{2,3},{3,2},{4,5},{5,4},{6,7},{7,6},{8,9},{9,8},{10,11... | collective-permute-start | bytes 196616 | tf_op jit(solution)/shard_map/ppermute | solution.py:316

commit v8 on v6

--- a/solution.py
+++ b/solution.py
@@ -184,7 +184,7 @@
             for i in range(window):
                 place(i, date * window + i, f)
 
-    chunk = max(1, 128 // dates)
+    chunk = max(1, 256 // dates)
 
     for step in range(STEPS):
         if plan.compact:
@@ -204,7 +204,7 @@
         def advance(r, n, row_in):
             current, following = old_ref[rows(r, n)], old_ref[rows(r + 1, n)]
             difference = jnp.dot(current.astype(jnp.bfloat16), onward, preferred_element_type=jnp.float32)
-            col_flux = (weights(col_ref, r, n) * phi(difference)).astype(jnp.bfloat16)
+            col_flux = weights(col_ref, r, n).astype(jnp.bfloat16) * phi(difference.astype(jnp.bfloat16))
             row_flux = weights(row_ref, r + 1, n) * phi(following - current)
             if n > 1:
                 row_before = jnp.concatenate([row_in, row_flux[:-dates]], axis=0)

time: 32 us -> 31.9 us (level)
  no operation moved by 1% of the time
where the time goes in v8:
time: 31.9 us; the launch traced here: 31.5 us
  blocking collectives  17.8 us (56%)
  Pallas kernels  5.12 us (16%)
  waiting for transfers between devices  4.56 us (14%)
  starting transfers between devices  3.38 us (11%)
  between operations  0.68 us (2%)
    all_to_all x1, blocking collectives, local(): got = lax.all_to_all(send, 'dates', split_axis=0, concat_axis=0, tiled=True)  17.8 us
    ppermute x5, waiting for transfers between devices, swap(): return lax.ppermute(x, 'dates', [(i, i ^ bits) for i in range(count)])  4.56 us
    ppermute x5, starting transfers between devices, swap(): return lax.ppermute(x, 'dates', [(i, i ^ bits) for i in range(count)])  3.38 us
    pallas_call x1, Pallas kernels, local(): pl.pallas_call(functools.partial(diffuse_kernel, plan), out_shape=(shape(...  2.57 us
    pallas_call x1, Pallas kernels, local(): pl.pallas_call(functools.partial(anomaly_kernel, plan), out_shape=shape(d...  1.47 us
    pallas_call x1, Pallas kernels, local(): pl.pallas_call(functools.partial(finish_kernel, plan), out_shape=(shape(d...  0.7 us
  transfers between devices with their start and end apart: 5, of which 3 were waited for; matrix products, arithmetic and copies ran while one was open for 0% of the time, Pallas kernels for 1%

profile of v8, /device:TPU:0, one launch (start us, length us, event | category | flops | bytes accessed | tf_op | source)
XLA Modules:
  0.0 31.5 jit_solution(5561998192051385111)
XLA Ops:
  0.6 1.5 %shard_map.50 = bf16[16,72,128]{2,1,0:T(8,128)(2,1)S(1)} custom-call(bf16[2,4,64,128]{3,2,1,0:T(8,128)(2,1)} %scenes_hbm.1, s32[2,64,128]{2,1,0:T(8,128)} %mask_hbm.1, s32[64,128]{1,0:T(8,128)} %region_ref.1), custom_call_target="tpu_custom_call" | custom-call | tf_op jit(solution)/shard_map/pallas_call | solution.py:333
  2.1 0.0 copy-start
  2.1 17.8 %all_to_all.5.got_ref = bf16[16,72,128]{2,1,0:T(8,128)(2,1)S(1)} all-to-all(bf16[16,72,128]{2,1,0:T(8,128)(2,1)S(1)} %shard_map.50), channel_id=1, replica_groups=mesh['groups'=2,'dates'=16] {'dates'}, dimensions={0} | all-to-all | bytes 589824 | tf_op jit(solution)/shard_map/all_to_all | solution.py:347
  19.9 0.0 copy-done
  19.9 2.6 %shard_map.51 = (f32[32,32]{1,0:T(8,128)S(1)}, f32[1184,128]{1,0:T(8,128)S(1)}) custom-call(bf16[16,72,128]{2,1,0:T(8,128)(2,1)S(1)} %all_to_all.5.got_ref, s32[64,128]{1,0:T(8,128)S(1)} %copy-done), custom_call_target="tpu_custom_call" | custom-call | tf_op jit(solution)/shard_map/pallas_call | solution.py:348
  22.5 0.0 collective-permute-start.2
  22.5 0.4 %shard_map.52 = (bf16[64,4,128]{2,1,0:T(4,128)(2,1)S(1)}, bf16[64,4,128]{2,1,0:T(4,128)(2,1)S(1)}) custom-call(f32[1184,128]{1,0:T(8,128)S(1)} %get-tuple-element.6.field_ref), custom_call_target="tpu_custom_call" | custom-call | flops 65536 | bytes 262144 | tf_op jit(solution)/shard_map/pallas_call | solution.py:365
  22.8 0.8 %collective-permute-done.2.got_ref = f32[32,32]{1,0:T(8,128)S(1)} collective-permute-done((f32[32,32]{1,0:T(8,128)S(1)}, f32[32,32]{1,0:T(8,128)S(1)}, u32[]{:S(2)}, u32[]{:S(2)}) %collective-permute-start.2) | collective-permute-done | bytes 4128 | tf_op jit(solution)/shard_map/ppermute | solution.py:315
  23.7 0.3 collective-permute-start.3
  23.9 1.5 %collective-permute-start = (bf16[64,4,128]{2,1,0:T(4,128)(2,1)S(1)}, bf16[64,4,128]{2,1,0:T(4,128)(2,1)S(1)}, u32[]{:S(2)}, u32[]{:S(2)}) collective-permute-start(bf16[64,4,128]{2,1,0:T(4,128)(2,1)S(1)} %get-tuple-element.8.message_ref), channel_id=1, source_target_pairs={{0,3},{1,2},{2,1},{3,0},{4,7},{5,6},{6,5},{7,4},{8,11},{9,10},{10,... | collective-permute-start | bytes 196616 | tf_op jit(solution)/shard_map/ppermute | solution.py:315
  25.4 1.4 %collective-permute-done.3 = f32[32,32]{1,0:T(8,128)S(1)} collective-permute-done((f32[32,32]{1,0:T(8,128)S(1)}, f32[32,32]{1,0:T(8,128)S(1)}, u32[]{:S(2)}, u32[]{:S(2)}) %collective-permute-start.3) | collective-permute-done | bytes 4128 | tf_op jit(solution)/shard_map/ppermute | solution.py:315
  26.8 1.5 %collective-permute-start.4 = (f32[2,32]{1,0:T(2,128)S(1)}, f32[2,32]{1,0:T(2,128)S(1)}, u32[]{:S(2)}, u32[]{:S(2)}) collective-permute-start(f32[2,32]{1,0:T(2,128)S(1)} %get-tuple-element.10), channel_id=1, source_target_pairs={{0,9},{1,8},{2,11},{3,10},{4,13},{5,12},{6,15},{7,14},{8,1},{9,0},... | collective-permute-start | bytes 776 | tf_op jit(solution)/shard_map/ppermute | solution.py:315
  28.4 0.0 collective-permute-done.got_ref.first_ref
  28.4 0.1 collective-permute-start.1
  28.5 2.3 %collective-permute-done.4.other_ref = f32[2,32]{1,0:T(2,128)S(1)} collective-permute-done((f32[2,32]{1,0:T(2,128)S(1)}, f32[2,32]{1,0:T(2,128)S(1)}, u32[]{:S(2)}, u32[]{:S(2)}) %collective-permute-start.4) | collective-permute-done | bytes 288 | tf_op jit(solution)/shard_map/ppermute | solution.py:315
  30.8 0.0 collective-permute-done.1.second_ref
  30.8 0.7 %shard_map.56 = (bf16[32,4,4,128]{3,2,1,0:T(4,128)(2,1)}, f32[2,32]{1,0:T(2,128)}) custom-call(bf16[64,4,128]{2,1,0:T(4,128)(2,1)S(1)} %get-tuple-element.7.rest_ref, bf16[64,4,128]{2,1,0:T(4,128)(2,1)S(1)} %collective-permute-done.got_ref.first_ref, bf16[64,4,128]{2,1,0:T(4,128)(2,1)S(1)} %collective-permute-done.1.second_ref, f32[2,32]{1,0:T(2,128)S(1)} %shard_map.55.sim_ref), custom_call_target="tpu_custom_call" | custom-call | flops 65536 | bytes 262144 | tf_op jit(solution)/shard_map/pallas_call | solution.py:410
  (5 shorter events, 0.0 us)
Async XLA Ops:
  2.1 17.8 %copy-start = (s32[64,128]{1,0:T(8,128)S(1)}, s32[64,128]{1,0:T(8,128)}, u32[]{:S(2)}) copy-start(s32[64,128]{1,0:T(8,128)} %region_ref.1) | copy-start | bytes 98308
  22.5 1.2 %collective-permute-start.2 = (f32[32,32]{1,0:T(8,128)S(1)}, f32[32,32]{1,0:T(8,128)S(1)}, u32[]{:S(2)}, u32[]{:S(2)}) collective-permute-start(f32[32,32]{1,0:T(8,128)S(1)} %get-tuple-element.9.gram_ref), channel_id=1, source_target_pairs={{0,1},{1,0},{2,3},{3,2},{4,5},{5,4},{6,7},{7,6},{8,9},{9,8},{10,11... | collective-permute-start | bytes 12296 | tf_op jit(solution)/shard_map/ppermute | solution.py:315
  23.7 3.2 %collective-permute-start.3 = (f32[32,32]{1,0:T(8,128)S(1)}, f32[32,32]{1,0:T(8,128)S(1)}, u32[]{:S(2)}, u32[]{:S(2)}) collective-permute-start(f32[32,32]{1,0:T(8,128)S(1)} %shard_map.54), channel_id=1, source_target_pairs={{0,3},{1,2},{2,1},{3,0},{4,7},{5,6},{6,5},{7,4},{8,11},{9,10},{10,... | collective-permute-start | bytes 12296 | tf_op jit(solution)/shard_map/ppermute | solution.py:315
  23.9 4.5 %collective-permute-start = (bf16[64,4,128]{2,1,0:T(4,128)(2,1)S(1)}, bf16[64,4,128]{2,1,0:T(4,128)(2,1)S(1)}, u32[]{:S(2)}, u32[]{:S(2)}) collective-permute-start(bf16[64,4,128]{2,1,0:T(4,128)(2,1)S(1)} %get-tuple-element.8.message_ref), channel_id=1, source_target_pairs={{0,3},{1,2},{2,1},{3,0},{4,7},{5,6},{6,5},{7,4},{8,11},{9,10},{10,... | collective-permute-start | bytes 196616 | tf_op jit(solution)/shard_map/ppermute | solution.py:315
  26.8 4.0 %collective-permute-start.4 = (f32[2,32]{1,0:T(2,128)S(1)}, f32[2,32]{1,0:T(2,128)S(1)}, u32[]{:S(2)}, u32[]{:S(2)}) collective-permute-start(f32[2,32]{1,0:T(2,128)S(1)} %get-tuple-element.10), channel_id=1, source_target_pairs={{0,9},{1,8},{2,11},{3,10},{4,13},{5,12},{6,15},{7,14},{8,1},{9,0},... | collective-permute-start | bytes 776 | tf_op jit(solution)/shard_map/ppermute | solution.py:315
  28.4 2.4 %collective-permute-start.1 = (bf16[64,4,128]{2,1,0:T(4,128)(2,1)S(1)}, bf16[64,4,128]{2,1,0:T(4,128)(2,1)S(1)}, u32[]{:S(2)}, u32[]{:S(2)}) collective-permute-start(bf16[64,4,128]{2,1,0:T(4,128)(2,1)S(1)} %shard_map.53), channel_id=1, source_target_pairs={{0,1},{1,0},{2,3},{3,2},{4,5},{5,4},{6,7},{7,6},{8,9},{9,8},{10,11... | collective-permute-start | bytes 196616 | tf_op jit(solution)/shard_map/ppermute | solution.py:315

commit v9 on v6

--- a/solution.py
+++ b/solution.py
@@ -184,7 +184,7 @@
             for i in range(window):
                 place(i, date * window + i, f)
 
-    chunk = max(1, 128 // dates)
+    chunk = max(1, 384 // dates)
 
     for step in range(STEPS):
         if plan.compact:

time: 32 us -> 32 us (level)
  no operation moved by 1% of the time
where the time goes in v9:
time: 32 us; the launch traced here: 31.6 us
  blocking collectives  17.8 us (56%)
  Pallas kernels  5.16 us (16%)
  waiting for transfers between devices  4.56 us (14%)
  starting transfers between devices  3.37 us (11%)
  between operations  0.68 us (2%)
    all_to_all x1, blocking collectives, local(): got = lax.all_to_all(send, 'dates', split_axis=0, concat_axis=0, tiled=True)  17.8 us
    ppermute x5, waiting for transfers between devices, swap(): return lax.ppermute(x, 'dates', [(i, i ^ bits) for i in range(count)])  4.56 us
    ppermute x5, starting transfers between devices, swap(): return lax.ppermute(x, 'dates', [(i, i ^ bits) for i in range(count)])  3.37 us
    pallas_call x1, Pallas kernels, local(): pl.pallas_call(functools.partial(diffuse_kernel, plan), out_shape=(shape(...  2.61 us
    pallas_call x1, Pallas kernels, local(): pl.pallas_call(functools.partial(anomaly_kernel, plan), out_shape=shape(d...  1.47 us
    pallas_call x1, Pallas kernels, local(): pl.pallas_call(functools.partial(finish_kernel, plan), out_shape=(shape(d...  0.7 us
  transfers between devices with their start and end apart: 5, of which 3 were waited for; matrix products, arithmetic and copies ran while one was open for 0% of the time, Pallas kernels for 1%

profile of v9, /device:TPU:0, one launch (start us, length us, event | category | flops | bytes accessed | tf_op | source)
XLA Modules:
  0.0 31.6 jit_solution(17896132311819761036)
XLA Ops:
  0.6 1.5 %shard_map.50 = bf16[16,72,128]{2,1,0:T(8,128)(2,1)S(1)} custom-call(bf16[2,4,64,128]{3,2,1,0:T(8,128)(2,1)} %scenes_hbm.1, s32[2,64,128]{2,1,0:T(8,128)} %mask_hbm.1, s32[64,128]{1,0:T(8,128)} %region_ref.1), custom_call_target="tpu_custom_call" | custom-call | tf_op jit(solution)/shard_map/pallas_call | solution.py:333
  2.1 0.0 copy-start
  2.1 17.8 %all_to_all.5.got_ref = bf16[16,72,128]{2,1,0:T(8,128)(2,1)S(1)} all-to-all(bf16[16,72,128]{2,1,0:T(8,128)(2,1)S(1)} %shard_map.50), channel_id=1, replica_groups=mesh['groups'=2,'dates'=16] {'dates'}, dimensions={0} | all-to-all | bytes 589824 | tf_op jit(solution)/shard_map/all_to_all | solution.py:347
  19.9 0.0 copy-done
  19.9 2.6 %shard_map.51 = (f32[32,32]{1,0:T(8,128)S(1)}, f32[1184,128]{1,0:T(8,128)S(1)}) custom-call(bf16[16,72,128]{2,1,0:T(8,128)(2,1)S(1)} %all_to_all.5.got_ref, s32[64,128]{1,0:T(8,128)S(1)} %copy-done), custom_call_target="tpu_custom_call" | custom-call | tf_op jit(solution)/shard_map/pallas_call | solution.py:348
  22.5 0.0 collective-permute-start.2
  22.5 0.4 %shard_map.52 = (bf16[64,4,128]{2,1,0:T(4,128)(2,1)S(1)}, bf16[64,4,128]{2,1,0:T(4,128)(2,1)S(1)}) custom-call(f32[1184,128]{1,0:T(8,128)S(1)} %get-tuple-element.6.field_ref), custom_call_target="tpu_custom_call" | custom-call | flops 65536 | bytes 262144 | tf_op jit(solution)/shard_map/pallas_call | solution.py:365
  22.9 0.8 %collective-permute-done.2.got_ref = f32[32,32]{1,0:T(8,128)S(1)} collective-permute-done((f32[32,32]{1,0:T(8,128)S(1)}, f32[32,32]{1,0:T(8,128)S(1)}, u32[]{:S(2)}, u32[]{:S(2)}) %collective-permute-start.2) | collective-permute-done | bytes 4128 | tf_op jit(solution)/shard_map/ppermute | solution.py:315
  23.7 0.3 collective-permute-start.3
  24.0 1.5 %collective-permute-start = (bf16[64,4,128]{2,1,0:T(4,128)(2,1)S(1)}, bf16[64,4,128]{2,1,0:T(4,128)(2,1)S(1)}, u32[]{:S(2)}, u32[]{:S(2)}) collective-permute-start(bf16[64,4,128]{2,1,0:T(4,128)(2,1)S(1)} %get-tuple-element.8.message_ref), channel_id=1, source_target_pairs={{0,3},{1,2},{2,1},{3,0},{4,7},{5,6},{6,5},{7,4},{8,11},{9,10},{10,... | collective-permute-start | bytes 196616 | tf_op jit(solution)/shard_map/ppermute | solution.py:315
  25.5 1.4 %collective-permute-done.3 = f32[32,32]{1,0:T(8,128)S(1)} collective-permute-done((f32[32,32]{1,0:T(8,128)S(1)}, f32[32,32]{1,0:T(8,128)S(1)}, u32[]{:S(2)}, u32[]{:S(2)}) %collective-permute-start.3) | collective-permute-done | bytes 4128 | tf_op jit(solution)/shard_map/ppermute | solution.py:315
  26.9 1.5 %collective-permute-start.4 = (f32[2,32]{1,0:T(2,128)S(1)}, f32[2,32]{1,0:T(2,128)S(1)}, u32[]{:S(2)}, u32[]{:S(2)}) collective-permute-start(f32[2,32]{1,0:T(2,128)S(1)} %get-tuple-element.10), channel_id=1, source_target_pairs={{0,9},{1,8},{2,11},{3,10},{4,13},{5,12},{6,15},{7,14},{8,1},{9,0},... | collective-permute-start | bytes 776 | tf_op jit(solution)/shard_map/ppermute | solution.py:315
  28.4 0.0 collective-permute-done.got_ref.first_ref
  28.4 0.1 collective-permute-start.1
  28.5 2.3 %collective-permute-done.4.other_ref = f32[2,32]{1,0:T(2,128)S(1)} collective-permute-done((f32[2,32]{1,0:T(2,128)S(1)}, f32[2,32]{1,0:T(2,128)S(1)}, u32[]{:S(2)}, u32[]{:S(2)}) %collective-permute-start.4) | collective-permute-done | bytes 288 | tf_op jit(solution)/shard_map/ppermute | solution.py:315
  30.8 0.0 collective-permute-done.1.second_ref
  30.9 0.7 %shard_map.56 = (bf16[32,4,4,128]{3,2,1,0:T(4,128)(2,1)}, f32[2,32]{1,0:T(2,128)}) custom-call(bf16[64,4,128]{2,1,0:T(4,128)(2,1)S(1)} %get-tuple-element.7.rest_ref, bf16[64,4,128]{2,1,0:T(4,128)(2,1)S(1)} %collective-permute-done.got_ref.first_ref, bf16[64,4,128]{2,1,0:T(4,128)(2,1)S(1)} %collective-permute-done.1.second_ref, f32[2,32]{1,0:T(2,128)S(1)} %shard_map.55.sim_ref), custom_call_target="tpu_custom_call" | custom-call | flops 65536 | bytes 262144 | tf_op jit(solution)/shard_map/pallas_call | solution.py:410
  (5 shorter events, 0.0 us)
Async XLA Ops:
  2.1 17.8 %copy-start = (s32[64,128]{1,0:T(8,128)S(1)}, s32[64,128]{1,0:T(8,128)}, u32[]{:S(2)}) copy-start(s32[64,128]{1,0:T(8,128)} %region_ref.1) | copy-start | bytes 98308
  22.5 1.2 %collective-permute-start.2 = (f32[32,32]{1,0:T(8,128)S(1)}, f32[32,32]{1,0:T(8,128)S(1)}, u32[]{:S(2)}, u32[]{:S(2)}) collective-permute-start(f32[32,32]{1,0:T(8,128)S(1)} %get-tuple-element.9.gram_ref), channel_id=1, source_target_pairs={{0,1},{1,0},{2,3},{3,2},{4,5},{5,4},{6,7},{7,6},{8,9},{9,8},{10,11... | collective-permute-start | bytes 12296 | tf_op jit(solution)/shard_map/ppermute | solution.py:315
  23.7 3.2 %collective-permute-start.3 = (f32[32,32]{1,0:T(8,128)S(1)}, f32[32,32]{1,0:T(8,128)S(1)}, u32[]{:S(2)}, u32[]{:S(2)}) collective-permute-start(f32[32,32]{1,0:T(8,128)S(1)} %shard_map.54), channel_id=1, source_target_pairs={{0,3},{1,2},{2,1},{3,0},{4,7},{5,6},{6,5},{7,4},{8,11},{9,10},{10,... | collective-permute-start | bytes 12296 | tf_op jit(solution)/shard_map/ppermute | solution.py:315
  24.0 4.5 %collective-permute-start = (bf16[64,4,128]{2,1,0:T(4,128)(2,1)S(1)}, bf16[64,4,128]{2,1,0:T(4,128)(2,1)S(1)}, u32[]{:S(2)}, u32[]{:S(2)}) collective-permute-start(bf16[64,4,128]{2,1,0:T(4,128)(2,1)S(1)} %get-tuple-element.8.message_ref), channel_id=1, source_target_pairs={{0,3},{1,2},{2,1},{3,0},{4,7},{5,6},{6,5},{7,4},{8,11},{9,10},{10,... | collective-permute-start | bytes 196616 | tf_op jit(solution)/shard_map/ppermute | solution.py:315
  26.9 4.0 %collective-permute-start.4 = (f32[2,32]{1,0:T(2,128)S(1)}, f32[2,32]{1,0:T(2,128)S(1)}, u32[]{:S(2)}, u32[]{:S(2)}) collective-permute-start(f32[2,32]{1,0:T(2,128)S(1)} %get-tuple-element.10), channel_id=1, source_target_pairs={{0,9},{1,8},{2,11},{3,10},{4,13},{5,12},{6,15},{7,14},{8,1},{9,0},... | collective-permute-start | bytes 776 | tf_op jit(solution)/shard_map/ppermute | solution.py:315
  28.4 2.4 %collective-permute-start.1 = (bf16[64,4,128]{2,1,0:T(4,128)(2,1)S(1)}, bf16[64,4,128]{2,1,0:T(4,128)(2,1)S(1)}, u32[]{:S(2)}, u32[]{:S(2)}) collective-permute-start(bf16[64,4,128]{2,1,0:T(4,128)(2,1)S(1)} %shard_map.53), channel_id=1, source_target_pairs={{0,1},{1,0},{2,3},{3,2},{4,5},{5,4},{6,7},{7,6},{8,9},{9,8},{10,11... | collective-permute-start | bytes 196616 | tf_op jit(solution)/shard_map/ppermute | solution.py:315
